TPU v7x, 128 devices: a whole 4x4x4 slice. The times are simulated.
128 devices in a mesh: img: 128 (over x, z, y, core).
Axes of the slice: x: 4, y: 4, z: 4, core: 2. Of those that a mesh axis runs over, the one named last changes fastest.
Arguments:
- queries: bfloat16 [49152, 1024], P('img'), may hold values from -10 to 10
- keys: bfloat16 [49152, 1024], P('img'), may hold values from -10 to 10
- values: bfloat16 [49152, 1024], P('img'), may hold values from -6 to 6
- out_grad: bfloat16 [49152, 1024], P('img'), may hold values from -6 to 6
- image_ids: int32 [49152], P('img'), may hold values from 0 to 127, never falling along the last dimension, each value on 1 to 1152 neighbouring positions
Outputs:
- attended: bfloat16 [49152, 1024], P('img')
- query_grad: bfloat16 [49152, 1024], P('img')
- key_grad: bfloat16 [49152, 1024], P('img')
- value_grad: bfloat16 [49152, 1024], P('img')
Inputs may be any that keep to these rules, and one draw needn't show every extreme that they name: `image_ids`: the regions of one image stand in consecutive rows, and ids rise along the rows; an image has 1 to 1152 regions, and some image has exactly 1152.
All inputs are finite; a program needn't handle non-finite values.
Results may differ from a plain program's by a relative error of at most 0.0069.
Values may be sent and summed in bfloat16 or wider, within the bound.
No kernel may reach another device: no remote copies, remote signals or barrier semaphores. Data moves between devices by JAX's collectives and lax.ppermute only.
A program may use at most 192 MiB of HBM per device.

v0:
```python
import math

import jax
import jax.numpy as jnp
from jax import lax
from jax.sharding import PartitionSpec as P

D = 1024
HEADS = 16
REACH = 3


def shifted(value, axis, steps):
    count = lax.axis_size(axis)
    leading, last = (max(0, -steps), min(count, count - steps))
    return lax.ppermute(value, axis, [(source, source + steps) for source in range(leading, last)])


def attend_pairs(query_rows, key_rows, value_rows, grad_rows, query_tags, key_tags):
    row_count = query_rows.shape[0]
    width = key_rows.shape[0]
    head_dim = D // HEADS
    pair_cols = 2 * head_dim
    score_scale = 1.0 / math.sqrt(head_dim)
    same_image = (query_tags[:, None] == key_tags[None, :])[None]

    def turn(pair_index, carry):
        attended, query_grad, key_grad, value_grad, peaks, totals, deltas = carry
        start = pair_index * pair_cols
        query_cols = lax.dynamic_slice_in_dim(query_rows, start, pair_cols, 1).reshape(
            row_count, 2, head_dim
        )
        key_cols = lax.dynamic_slice_in_dim(key_rows, start, pair_cols, 1).reshape(
            width, 2, head_dim
        )
        value_cols = lax.dynamic_slice_in_dim(value_rows, start, pair_cols, 1).reshape(
            width, 2, head_dim
        )
        grad_cols = lax.dynamic_slice_in_dim(grad_rows, start, pair_cols, 1).reshape(
            row_count, 2, head_dim
        )
        scores = (
            jnp.einsum("rhd,whd->hrw", query_cols, key_cols, preferred_element_type=jnp.float32)
            * score_scale
        )
        scores = jnp.where(same_image, scores, -1e30)
        peak = jnp.max(scores, axis=-1, keepdims=True)
        weights = jnp.exp(scores - peak)
        total = jnp.sum(weights, axis=-1, keepdims=True)
        probs = weights / total
        probs_b = probs.astype(jnp.bfloat16)
        output = jnp.einsum("hrw,whd->rhd", probs_b, value_cols, preferred_element_type=jnp.float32)
        dprobs = jnp.einsum(
            "rhd,whd->hrw", grad_cols, value_cols, preferred_element_type=jnp.float32
        )
        row_delta = jnp.sum(probs * dprobs, axis=-1, keepdims=True)
        dscores_b = (probs * (dprobs - row_delta)).astype(jnp.bfloat16)
        query_part = (
            jnp.einsum("hrw,whd->rhd", dscores_b, key_cols, preferred_element_type=jnp.float32)
            * score_scale
        )
        attended = lax.dynamic_update_slice_in_dim(
            attended, output.reshape(row_count, pair_cols).astype(jnp.bfloat16), start, 1
        )
        query_grad = lax.dynamic_update_slice_in_dim(
            query_grad, query_part.reshape(row_count, pair_cols).astype(jnp.bfloat16), start, 1
        )
        key_part = (
            jnp.einsum("hrw,rhd->whd", dscores_b, query_cols, preferred_element_type=jnp.float32)
            * score_scale
        )
        value_part = jnp.einsum(
            "hrw,rhd->whd", probs_b, grad_cols, preferred_element_type=jnp.float32
        )
        key_grad = lax.dynamic_update_slice_in_dim(
            key_grad, key_part.reshape(width, pair_cols), start, 1
        )
        value_grad = lax.dynamic_update_slice_in_dim(
            value_grad, value_part.reshape(width, pair_cols), start, 1
        )
        head_start = pair_index * 2
        peaks = lax.dynamic_update_slice_in_dim(peaks, peak[:, :, 0], head_start, 0)
        totals = lax.dynamic_update_slice_in_dim(totals, total[:, :, 0], head_start, 0)
        deltas = lax.dynamic_update_slice_in_dim(deltas, row_delta[:, :, 0], head_start, 0)
        return (attended, query_grad, key_grad, value_grad, peaks, totals, deltas)

    initial = (
        jnp.zeros((row_count, D), jnp.bfloat16),
        jnp.zeros((row_count, D), jnp.bfloat16),
        jnp.zeros((width, D), jnp.float32),
        jnp.zeros((width, D), jnp.float32),
        jnp.zeros((HEADS, row_count), jnp.float32),
        jnp.zeros((HEADS, row_count), jnp.float32),
        jnp.zeros((HEADS, row_count), jnp.float32),
    )
    return lax.fori_loop(0, HEADS // 2, turn, initial)


def fetch_near(block, distance):
    return shifted((block[0], block[1], block[2]), "img", distance)


def return_near(partial_value, distance):
    return shifted((partial_value[0], partial_value[1]), "img", distance)


def shards(queries, keys, values, out_grad, image_ids):
    row_count = queries.shape[0]
    image_tags = image_ids + 1
    own_block = (keys, values, image_tags)
    lower_parts = []
    upper_parts = []
    for offset in range(1, REACH + 1):
        lower_parts.insert(0, fetch_near(own_block, offset))
        upper_parts.append(fetch_near(own_block, -offset))
    all_parts = lower_parts + [own_block] + upper_parts
    window = tuple(
        (jnp.concatenate([piece[member] for piece in all_parts], 0) for member in range(3))
    )
    key_window, value_window, tag_window = window

    def attend_full():
        return attend_pairs(queries, key_window, value_window, out_grad, image_tags, tag_window)

    def attend_near():
        first_row = (REACH - 1) * row_count
        last_row = (REACH + 2) * row_count
        result = attend_pairs(
            queries,
            key_window[first_row:last_row],
            value_window[first_row:last_row],
            out_grad,
            image_tags,
            tag_window[first_row:last_row],
        )
        attended, query_grad, key_grad, value_grad, peaks, totals, deltas = result
        padding = ((first_row, key_window.shape[0] - last_row), (0, 0))
        key_grad = jnp.pad(key_grad, padding)
        value_grad = jnp.pad(value_grad, padding)
        return (attended, query_grad, key_grad, value_grad, peaks, totals, deltas)

    far_needed = jnp.logical_or(
        tag_window[(REACH - 1) * row_count - 1] == image_tags[0],
        tag_window[(REACH + 2) * row_count] == image_tags[row_count - 1],
    )
    result = lax.cond(far_needed, attend_full, attend_near)
    attended, query_grad, key_part, value_part, peaks, totals, deltas = result
    own_start = REACH * row_count
    key_total = key_part[own_start : own_start + row_count]
    value_total = value_part[own_start : own_start + row_count]
    for offset in range(-REACH, REACH + 1):
        if offset != 0:
            begin = (offset + REACH) * row_count
            key_back, value_back = return_near(
                (key_part[begin : begin + row_count], value_part[begin : begin + row_count]), offset
            )
            key_total = key_total + key_back
            value_total = value_total + value_back
    return (attended, query_grad, key_total.astype(jnp.bfloat16), value_total.astype(jnp.bfloat16))


def solution(mesh):
    in_specs = (P("img", None), P("img", None), P("img", None), P("img", None), P("img"))
    out_specs = (P("img", None), P("img", None), P("img", None), P("img", None))
    return jax.shard_map(shards, mesh=mesh, in_specs=in_specs, out_specs=out_specs, check_vma=False)
```

profile of v0, /device:TPU:124, one launch (start us, length us, event | category | flops | bytes accessed | tf_op | source)
XLA Modules:
  0.0 676.9 jit_solution(10681163148079595898)
XLA Ops:
  8.2 8.4 %collective-permute-start.14 = (s32[384]{0:T(512)S(1)}, s32[384]{0:T(512)S(1)}, u32[]{:S(2)}, u32[]{:S(2)}) collective-permute-start(s32[384]{0:T(512)S(1)} %broadcast_add_fusion), channel_id=1, source_target_pairs={{0,3},{1,4},{2,5},{3,6},{4,7},{5,8},{6,9},{7,10},{8,11},{9,12},{10... | collective-permute-start | bytes 4616 | tf_op jit(solution)/shard_map/ppermute | solution.py:16
  46.7 15.1 %collective-permute-start.10 = (bf16[384,1024]{0,1:T(8,128)(2,1)S(1)}, bf16[384,1024]{0,1:T(8,128)(2,1)S(1)}, u32[]{:S(2)}, u32[]{:S(2)}) collective-permute-start(bf16[384,1024]{0,1:T(8,128)(2,1)S(1)} %copy.16), channel_id=1, source_target_pairs={{0,1},{1,2},{2,3},{3,4},{4,5},{5,6},{6,7},{7,8},{8,9},{9,10},{10,1... | collective-permute-start | bytes 2359304 | tf_op jit(solution)/shard_map/ppermute | solution.py:16
  62.9 13.8 %collective-permute-done.3 = bf16[384,1024]{0,1:T(8,128)(2,1)S(1)} collective-permute-done((bf16[384,1024]{0,1:T(8,128)(2,1)S(1)}, bf16[384,1024]{0,1:T(8,128)(2,1)S(1)}, u32[]{:S(2)}, u32[]{:S(2)}) %collective-permute-start.3) | collective-permute-done | bytes 786464 | tf_op jit(solution)/shard_map/ppermute | solution.py:16
  91.5 18.9 %collective-permute-done.9 = bf16[384,1024]{0,1:T(8,128)(2,1)S(1)} collective-permute-done((bf16[384,1024]{0,1:T(8,128)(2,1)S(1)}, bf16[384,1024]{0,1:T(8,128)(2,1)S(1)}, u32[]{:S(2)}, u32[]{:S(2)}) %collective-permute-start.9) | collective-permute-done | bytes 786464 | tf_op jit(solution)/shard_map/ppermute | solution.py:16
  113.3 10.9 %collective-permute-start.12 = (bf16[384,1024]{0,1:T(8,128)(2,1)S(1)}, bf16[384,1024]{0,1:T(8,128)(2,1)S(1)}, u32[]{:S(2)}, u32[]{:S(2)}) collective-permute-start(bf16[384,1024]{0,1:T(8,128)(2,1)S(1)} %copy.16), channel_id=1, source_target_pairs={{2,0},{3,1},{4,2},{5,3},{6,4},{7,5},{8,6},{9,7},{10,8},{11,9},{12,... | collective-permute-start | bytes 2359304 | tf_op jit(solution)/shard_map/ppermute | solution.py:16
  140.3 8.6 %collective-permute-done.11 = bf16[384,1024]{0,1:T(8,128)(2,1)S(1)} collective-permute-done((bf16[384,1024]{0,1:T(8,128)(2,1)S(1)}, bf16[384,1024]{0,1:T(8,128)(2,1)S(1)}, u32[]{:S(2)}, u32[]{:S(2)}) %collective-permute-start.11) | collective-permute-done | bytes 786464 | tf_op jit(solution)/shard_map/ppermute | solution.py:16
  149.8 33.0 %collective-permute-done.12 = bf16[384,1024]{0,1:T(8,128)(2,1)S(1)} collective-permute-done((bf16[384,1024]{0,1:T(8,128)(2,1)S(1)}, bf16[384,1024]{0,1:T(8,128)(2,1)S(1)}, u32[]{:S(2)}, u32[]{:S(2)}) %collective-permute-start.12) | collective-permute-done | bytes 786464 | tf_op jit(solution)/shard_map/ppermute | solution.py:16
  184.9 205.4 %conditional.1 = (bf16[384,1024]{0,1:T(8,128)(2,1)}, bf16[384,1024]{0,1:T(8,128)(2,1)}, f32[2688,1024]{0,1:T(8,128)}, f32[2688,1024]{0,1:T(8,128)}) conditional(s32[]{:T(128)} %bitcast, (bf16[2688,1024]{0,1:T(8,128)(2,1)}, bf16[2688,1024]{0,1:T(8,128)(2,1)}, s32[384]{0:T(512)S(1)}, s32[2688]{0:T(1024)S(1)}, bf16[384,1024]{1,0:T(8,128)(2,1)}, ...), branch_computations={%region_0.6_spmd, %region_6.12_spmd} | conditional | flops 2158813696 | bytes 127279744 | solution.py:146
  196.8 181.5 %while.38 = (s32[]{:T(128)}, bf16[384,1024]{0,1:T(8,128)(2,1)}, bf16[384,1024]{0,1:T(8,128)(2,1)}, f32[1152,1024]{0,1:T(8,128)}, f32[1152,1024]{0,1:T(8,128)}, /...) while((s32[]{:T(128)}, bf16[384,1024]{0,1:T(8,128)(2,1)}, ...), condition=%wide.region_5.5_spmd.clone, body=%wide.region_1.4_spmd.clone.sunk | while | flops 925290624 | bytes 56491444 | solution.py:96
  378.3 7.2 %pad.6 = f32[2688,1024]{0,1:T(8,128)} pad(f32[1152,1024]{0,1:T(8,128)} %get-tuple-element.358, f32[]{:T(128)} %constant.109.clone), padding=768_768x0_0 | pad | bytes 15728644 | tf_op jit(solution)/shard_map/cond/branch_0_fun/jit(_pad)/pad | solution.py:139
  390.3 12.1 %copy.27 = f32[2688,1024]{1,0:T(8,128)} copy(f32[2688,1024]{0,1:T(8,128)} %get-tuple-element.390) | data formatting | bytes 22020096 | tf_op jit(solution)/shard_map/cond | solution.py:146
  402.3 7.8 %fusion.47 = (f32[384,1024]{1,0:T(8,128)}, f32[384,1024]{1,0:T(8,128)}, f32[384,1024]{1,0:T(8,128)}, f32[384,1024]{1,0:T(8,128)}, f32[384,1024]{1,0:T(8,128)}, /*index=5*/f32[384,1024]{1,0:T(8,128)}) fusion(f32[2688,1024]{1,0:T(8,128)} %copy.27), kind=kLoop, calls=%fused_computation.98 | loop fusion | bytes 18874368 | tf_op jit(solution)/shard_map/slice | solution.py:155
  412.1 33.5 %collective-permute-start.23 = (f32[384,1024]{1,0:T(8,128)}, f32[384,1024]{1,0:T(8,128)}, u32[]{:S(2)}, u32[]{:S(2)}) collective-permute-start(f32[384,1024]{1,0:T(8,128)} %get-tuple-element.527), channel_id=1, source_target_pairs={{0,3},{1,4},{2,5},{3,6},{4,7},{5,8},{6,9},{7,10},{8,11},{9,12},{10... | collective-permute-start | bytes 4718600 | tf_op jit(solution)/shard_map/ppermute | solution.py:16
  445.6 22.5 %collective-permute-start.22 = (f32[384,1024]{1,0:T(8,128)}, f32[384,1024]{1,0:T(8,128)}, u32[]{:S(2)}, u32[]{:S(2)}) collective-permute-start(f32[384,1024]{1,0:T(8,128)} %get-tuple-element.528), channel_id=1, source_target_pairs={{0,2},{1,3},{2,4},{3,5},{4,6},{5,7},{6,8},{7,9},{8,10},{9,11},{10,... | collective-permute-start | bytes 4718600 | tf_op jit(solution)/shard_map/ppermute | solution.py:16
  473.7 12.1 %copy.34 = f32[2688,1024]{1,0:T(8,128)} copy(f32[2688,1024]{0,1:T(8,128)} %get-tuple-element.391) | data formatting | bytes 22020096 | tf_op jit(solution)/shard_map/cond | solution.py:146
  485.8 6.8 %fusion.46 = (f32[384,1024]{1,0:T(8,128)S(1)}, f32[384,1024]{1,0:T(8,128)}, f32[384,1024]{1,0:T(8,128)}, f32[384,1024]{1,0:T(8,128)}, f32[384,1024]{1,0:T(8,128)S(1)}, /*index=5*/f32[384,1024]{1,0:T(8,128)S(1)}) fusion(f32[2688,1024]{1,0:T(8,128)} %copy.34), kind=kLoop, calls=%fused_computation.97 | loop fusion | bytes 18874368 | tf_op jit(solution)/shard_map/slice | solution.py:155
  498.3 23.3 %collective-permute-done.22 = f32[384,1024]{1,0:T(8,128)} collective-permute-done((f32[384,1024]{1,0:T(8,128)}, f32[384,1024]{1,0:T(8,128)}, u32[]{:S(2)}, u32[]{:S(2)}) %collective-permute-start.22) | collective-permute-done | bytes 1572896 | tf_op jit(solution)/shard_map/ppermute | solution.py:16
  521.6 10.2 %collective-permute-start.29 = (f32[384,1024]{1,0:T(8,128)}, f32[384,1024]{1,0:T(8,128)}, u32[]{:S(2)}, u32[]{:S(2)}) collective-permute-start(f32[384,1024]{1,0:T(8,128)} %get-tuple-element.521), channel_id=1, source_target_pairs={{0,3},{1,4},{2,5},{3,6},{4,7},{5,8},{6,9},{7,10},{8,11},{9,12},{10... | collective-permute-start | bytes 4718600 | tf_op jit(solution)/shard_map/ppermute | solution.py:16
  531.8 41.0 %collective-permute-start.28 = (f32[384,1024]{1,0:T(8,128)}, f32[384,1024]{1,0:T(8,128)}, u32[]{:S(2)}, u32[]{:S(2)}) collective-permute-start(f32[384,1024]{1,0:T(8,128)} %get-tuple-element.522), channel_id=1, source_target_pairs={{0,2},{1,3},{2,4},{3,5},{4,6},{5,7},{6,8},{7,9},{8,10},{9,11},{10,... | collective-permute-start | bytes 4718600 | tf_op jit(solution)/shard_map/ppermute | solution.py:16
  574.8 7.6 %collective-permute-done.19 = f32[384,1024]{1,0:T(8,128)S(1)} collective-permute-done((f32[384,1024]{1,0:T(8,128)S(1)}, f32[384,1024]{1,0:T(8,128)S(1)}, u32[]{:S(2)}, u32[]{:S(2)}) %collective-permute-start.19) | collective-permute-done | bytes 1572896 | tf_op jit(solution)/shard_map/ppermute | solution.py:16
  584.3 13.5 %collective-permute-done.24 = f32[384,1024]{1,0:T(8,128)S(1)} collective-permute-done((f32[384,1024]{1,0:T(8,128)S(1)}, f32[384,1024]{1,0:T(8,128)S(1)}, u32[]{:S(2)}, u32[]{:S(2)}) %collective-permute-start.24) | collective-permute-done | bytes 1572896 | tf_op jit(solution)/shard_map/ppermute | solution.py:16
  604.3 6.2 fusion.43
  610.6 6.9 %collective-permute-done.28 = f32[384,1024]{1,0:T(8,128)} collective-permute-done((f32[384,1024]{1,0:T(8,128)}, f32[384,1024]{1,0:T(8,128)}, u32[]{:S(2)}, u32[]{:S(2)}) %collective-permute-start.28) | collective-permute-done | bytes 1572896 | tf_op jit(solution)/shard_map/ppermute | solution.py:16
  618.8 52.4 %collective-permute-done.25 = f32[384,1024]{1,0:T(8,128)} collective-permute-done((f32[384,1024]{1,0:T(8,128)S(1)}, f32[384,1024]{1,0:T(8,128)}, u32[]{:S(2)}, u32[]{:S(2)}) %collective-permute-start.25) | collective-permute-done | bytes 1572896 | tf_op jit(solution)/shard_map/ppermute | solution.py:16
  (349 shorter events, 300.6 us)
Async XLA Ops:
  3.9 30.6 %collective-permute-start.16 = (s32[384]{0:T(512)S(1)}, s32[384]{0:T(512)S(1)}, u32[]{:S(2)}, u32[]{:S(2)}) collective-permute-start(s32[384]{0:T(512)S(1)} %broadcast_add_fusion), channel_id=1, source_target_pairs={{1,0},{2,1},{3,2},{4,3},{5,4},{6,5},{7,6},{8,7},{9,8},{10,9},{11,1... | collective-permute-start | bytes 4616 | tf_op jit(solution)/shard_map/ppermute | solution.py:16
  25.8 54.5 %collective-permute-start.4 = (bf16[384,1024]{0,1:T(8,128)(2,1)S(1)}, bf16[384,1024]{0,1:T(8,128)(2,1)S(1)}, u32[]{:S(2)}, u32[]{:S(2)}) collective-permute-start(bf16[384,1024]{0,1:T(8,128)(2,1)S(1)} %copy.9), channel_id=1, source_target_pairs={{0,1},{1,2},{2,3},{3,4},{4,5},{5,6},{6,7},{7,8},{8,9},{9,10},{10,1... | collective-permute-start | bytes 2359304 | tf_op jit(solution)/shard_map/ppermute | solution.py:16
  27.9 48.8 %collective-permute-start.3 = (bf16[384,1024]{0,1:T(8,128)(2,1)S(1)}, bf16[384,1024]{0,1:T(8,128)(2,1)S(1)}, u32[]{:S(2)}, u32[]{:S(2)}) collective-permute-start(bf16[384,1024]{0,1:T(8,128)(2,1)S(1)} %copy.9), channel_id=1, source_target_pairs={{0,2},{1,3},{2,4},{3,5},{4,6},{5,7},{6,8},{7,9},{8,10},{9,11},{10,... | collective-permute-start | bytes 2359304 | tf_op jit(solution)/shard_map/ppermute | solution.py:16
  34.5 54.0 %collective-permute-start.8 = (bf16[384,1024]{0,1:T(8,128)(2,1)S(1)}, bf16[384,1024]{0,1:T(8,128)(2,1)S(1)}, u32[]{:S(2)}, u32[]{:S(2)}) collective-permute-start(bf16[384,1024]{0,1:T(8,128)(2,1)S(1)} %copy.16), channel_id=1, source_target_pairs={{0,3},{1,4},{2,5},{3,6},{4,7},{5,8},{6,9},{7,10},{8,11},{9,12},{10... | collective-permute-start | bytes 2359304 | tf_op jit(solution)/shard_map/ppermute | solution.py:16
  40.7 69.7 %collective-permute-start.9 = (bf16[384,1024]{0,1:T(8,128)(2,1)S(1)}, bf16[384,1024]{0,1:T(8,128)(2,1)S(1)}, u32[]{:S(2)}, u32[]{:S(2)}) collective-permute-start(bf16[384,1024]{0,1:T(8,128)(2,1)S(1)} %copy.16), channel_id=1, source_target_pairs={{0,2},{1,3},{2,4},{3,5},{4,6},{5,7},{6,8},{7,9},{8,10},{9,11},{10,... | collective-permute-start | bytes 2359304 | tf_op jit(solution)/shard_map/ppermute | solution.py:16
  46.7 66.6 %collective-permute-start.10 = (bf16[384,1024]{0,1:T(8,128)(2,1)S(1)}, bf16[384,1024]{0,1:T(8,128)(2,1)S(1)}, u32[]{:S(2)}, u32[]{:S(2)}) collective-permute-start(bf16[384,1024]{0,1:T(8,128)(2,1)S(1)} %copy.16), channel_id=1, source_target_pairs={{0,1},{1,2},{2,3},{3,4},{4,5},{5,6},{6,7},{7,8},{8,9},{9,10},{10,1... | collective-permute-start | bytes 2359304 | tf_op jit(solution)/shard_map/ppermute | solution.py:16
  76.7 48.6 %collective-permute-start.5 = (bf16[384,1024]{0,1:T(8,128)(2,1)S(1)}, bf16[384,1024]{0,1:T(8,128)(2,1)S(1)}, u32[]{:S(2)}, u32[]{:S(2)}) collective-permute-start(bf16[384,1024]{0,1:T(8,128)(2,1)S(1)} %copy.9), channel_id=1, source_target_pairs={{1,0},{2,1},{3,2},{4,3},{5,4},{6,5},{7,6},{8,7},{9,8},{10,9},{11,1... | collective-permute-start | bytes 2359304 | tf_op jit(solution)/shard_map/ppermute | solution.py:16
  80.3 53.1 %collective-permute-start.6 = (bf16[384,1024]{0,1:T(8,128)(2,1)S(1)}, bf16[384,1024]{0,1:T(8,128)(2,1)S(1)}, u32[]{:S(2)}, u32[]{:S(2)}) collective-permute-start(bf16[384,1024]{0,1:T(8,128)(2,1)S(1)} %copy.9), channel_id=1, source_target_pairs={{2,0},{3,1},{4,2},{5,3},{6,4},{7,5},{8,6},{9,7},{10,8},{11,9},{12,... | collective-permute-start | bytes 2359304 | tf_op jit(solution)/shard_map/ppermute | solution.py:16
  88.4 50.8 %collective-permute-start.7 = (bf16[384,1024]{0,1:T(8,128)(2,1)S(1)}, bf16[384,1024]{0,1:T(8,128)(2,1)S(1)}, u32[]{:S(2)}, u32[]{:S(2)}) collective-permute-start(bf16[384,1024]{0,1:T(8,128)(2,1)S(1)} %copy.9), channel_id=1, source_target_pairs={{3,0},{4,1},{5,2},{6,3},{7,4},{8,5},{9,6},{10,7},{11,8},{12,9},{13... | collective-permute-start | bytes 2359304 | tf_op jit(solution)/shard_map/ppermute | solution.py:16
  110.4 38.4 %collective-permute-start.11 = (bf16[384,1024]{0,1:T(8,128)(2,1)S(1)}, bf16[384,1024]{0,1:T(8,128)(2,1)S(1)}, u32[]{:S(2)}, u32[]{:S(2)}) collective-permute-start(bf16[384,1024]{0,1:T(8,128)(2,1)S(1)} %copy.16), channel_id=1, source_target_pairs={{1,0},{2,1},{3,2},{4,3},{5,4},{6,5},{7,6},{8,7},{9,8},{10,9},{11,1... | collective-permute-start | bytes 2359304 | tf_op jit(solution)/shard_map/ppermute | solution.py:16
  113.3 69.4 %collective-permute-start.12 = (bf16[384,1024]{0,1:T(8,128)(2,1)S(1)}, bf16[384,1024]{0,1:T(8,128)(2,1)S(1)}, u32[]{:S(2)}, u32[]{:S(2)}) collective-permute-start(bf16[384,1024]{0,1:T(8,128)(2,1)S(1)} %copy.16), channel_id=1, source_target_pairs={{2,0},{3,1},{4,2},{5,3},{6,4},{7,5},{8,6},{9,7},{10,8},{11,9},{12,... | collective-permute-start | bytes 2359304 | tf_op jit(solution)/shard_map/ppermute | solution.py:16
  125.3 58.5 %collective-permute-start.13 = (bf16[384,1024]{0,1:T(8,128)(2,1)S(1)}, bf16[384,1024]{0,1:T(8,128)(2,1)S(1)}, u32[]{:S(2)}, u32[]{:S(2)}) collective-permute-start(bf16[384,1024]{0,1:T(8,128)(2,1)S(1)} %copy.16), channel_id=1, source_target_pairs={{3,0},{4,1},{5,2},{6,3},{7,4},{8,5},{9,6},{10,7},{11,8},{12,9},{13... | collective-permute-start | bytes 2359304 | tf_op jit(solution)/shard_map/ppermute | solution.py:16
  410.2 82.5 %collective-permute-start.18 = (f32[384,1024]{1,0:T(8,128)}, f32[384,1024]{1,0:T(8,128)}, u32[]{:S(2)}, u32[]{:S(2)}) collective-permute-start(f32[384,1024]{1,0:T(8,128)} %get-tuple-element.526), channel_id=1, source_target_pairs={{3,0},{4,1},{5,2},{6,3},{7,4},{8,5},{9,6},{10,7},{11,8},{12,9},{13... | collective-permute-start | bytes 4718600 | tf_op jit(solution)/shard_map/ppermute | solution.py:16
  412.1 83.0 %collective-permute-start.23 = (f32[384,1024]{1,0:T(8,128)}, f32[384,1024]{1,0:T(8,128)}, u32[]{:S(2)}, u32[]{:S(2)}) collective-permute-start(f32[384,1024]{1,0:T(8,128)} %get-tuple-element.527), channel_id=1, source_target_pairs={{0,3},{1,4},{2,5},{3,6},{4,7},{5,8},{6,9},{7,10},{8,11},{9,12},{10... | collective-permute-start | bytes 4718600 | tf_op jit(solution)/shard_map/ppermute | solution.py:16
  445.6 76.0 %collective-permute-start.22 = (f32[384,1024]{1,0:T(8,128)}, f32[384,1024]{1,0:T(8,128)}, u32[]{:S(2)}, u32[]{:S(2)}) collective-permute-start(f32[384,1024]{1,0:T(8,128)} %get-tuple-element.528), channel_id=1, source_target_pairs={{0,2},{1,3},{2,4},{3,5},{4,6},{5,7},{6,8},{7,9},{8,10},{9,11},{10,... | collective-permute-start | bytes 4718600 | tf_op jit(solution)/shard_map/ppermute | solution.py:16
  468.1 63.7 %collective-permute-start.21 = (f32[384,1024]{1,0:T(8,128)}, f32[384,1024]{1,0:T(8,128)}, u32[]{:S(2)}, u32[]{:S(2)}) collective-permute-start(f32[384,1024]{1,0:T(8,128)} %get-tuple-element.529), channel_id=1, source_target_pairs={{0,1},{1,2},{2,3},{3,4},{4,5},{5,6},{6,7},{7,8},{8,9},{9,10},{10,1... | collective-permute-start | bytes 4718600 | tf_op jit(solution)/shard_map/ppermute | solution.py:16
  470.0 102.8 %collective-permute-start.20 = (f32[384,1024]{1,0:T(8,128)}, f32[384,1024]{1,0:T(8,128)}, u32[]{:S(2)}, u32[]{:S(2)}) collective-permute-start(f32[384,1024]{1,0:T(8,128)} %get-tuple-element.530), channel_id=1, source_target_pairs={{1,0},{2,1},{3,2},{4,3},{5,4},{6,5},{7,6},{8,7},{9,8},{10,9},{11,1... | collective-permute-start | bytes 4718600 | tf_op jit(solution)/shard_map/ppermute | solution.py:16
  492.6 89.8 %collective-permute-start.19 = (f32[384,1024]{1,0:T(8,128)S(1)}, f32[384,1024]{1,0:T(8,128)S(1)}, u32[]{:S(2)}, u32[]{:S(2)}) collective-permute-start(f32[384,1024]{1,0:T(8,128)S(1)} %copy-done.8), channel_id=1, source_target_pairs={{2,0},{3,1},{4,2},{5,3},{6,4},{7,5},{8,6},{9,7},{10,8},{11,9},{12,... | collective-permute-start | bytes 4718600 | tf_op jit(solution)/shard_map/ppermute | solution.py:16
  495.1 102.7 %collective-permute-start.24 = (f32[384,1024]{1,0:T(8,128)S(1)}, f32[384,1024]{1,0:T(8,128)S(1)}, u32[]{:S(2)}, u32[]{:S(2)}) collective-permute-start(f32[384,1024]{1,0:T(8,128)S(1)} %get-tuple-element.520), channel_id=1, source_target_pairs={{3,0},{4,1},{5,2},{6,3},{7,4},{8,5},{9,6},{10,7},{11,8},{12,9},{13... | collective-permute-start | bytes 4718600 | tf_op jit(solution)/shard_map/ppermute | solution.py:16
  521.6 89.0 %collective-permute-start.29 = (f32[384,1024]{1,0:T(8,128)}, f32[384,1024]{1,0:T(8,128)}, u32[]{:S(2)}, u32[]{:S(2)}) collective-permute-start(f32[384,1024]{1,0:T(8,128)} %get-tuple-element.521), channel_id=1, source_target_pairs={{0,3},{1,4},{2,5},{3,6},{4,7},{5,8},{6,9},{7,10},{8,11},{9,12},{10... | collective-permute-start | bytes 4718600 | tf_op jit(solution)/shard_map/ppermute | solution.py:16
  531.8 85.7 %collective-permute-start.28 = (f32[384,1024]{1,0:T(8,128)}, f32[384,1024]{1,0:T(8,128)}, u32[]{:S(2)}, u32[]{:S(2)}) collective-permute-start(f32[384,1024]{1,0:T(8,128)} %get-tuple-element.522), channel_id=1, source_target_pairs={{0,2},{1,3},{2,4},{3,5},{4,6},{5,7},{6,8},{7,9},{8,10},{9,11},{10,... | collective-permute-start | bytes 4718600 | tf_op jit(solution)/shard_map/ppermute | solution.py:16
  572.9 45.9 %collective-permute-start.27 = (f32[384,1024]{1,0:T(8,128)}, f32[384,1024]{1,0:T(8,128)}, u32[]{:S(2)}, u32[]{:S(2)}) collective-permute-start(f32[384,1024]{1,0:T(8,128)} %get-tuple-element.523), channel_id=1, source_target_pairs={{0,1},{1,2},{2,3},{3,4},{4,5},{5,6},{6,7},{7,8},{8,9},{9,10},{10,1... | collective-permute-start | bytes 4718600 | tf_op jit(solution)/shard_map/ppermute | solution.py:16
  582.4 36.4 %collective-permute-start.26 = (f32[384,1024]{1,0:T(8,128)S(1)}, f32[384,1024]{1,0:T(8,128)}, u32[]{:S(2)}, u32[]{:S(2)}) collective-permute-start(f32[384,1024]{1,0:T(8,128)S(1)} %get-tuple-element.524), channel_id=1, source_target_pairs={{1,0},{2,1},{3,2},{4,3},{5,4},{6,5},{7,6},{8,7},{9,8},{10,9},{11,1... | collective-permute-start | bytes 4718600 | tf_op jit(solution)/shard_map/ppermute | solution.py:16
  597.8 73.4 %collective-permute-start.25 = (f32[384,1024]{1,0:T(8,128)S(1)}, f32[384,1024]{1,0:T(8,128)}, u32[]{:S(2)}, u32[]{:S(2)}) collective-permute-start(f32[384,1024]{1,0:T(8,128)S(1)} %get-tuple-element.525), channel_id=1, source_target_pairs={{2,0},{3,1},{4,2},{5,3},{6,4},{7,5},{8,6},{9,7},{10,8},{11,9},{12,... | collective-permute-start | bytes 4718600 | tf_op jit(solution)/shard_map/ppermute | solution.py:16
  (75 other events, 395.8 us)
where the time goes:
time: 680 us; the launch traced here: 677 us
  starting transfers between devices  204 us (30%)
  waiting for transfers between devices  188 us (28%)
  local copies, waits for them, and re-layouts  151 us (22%)
  matrix products  103 us (15%)
  other arithmetic  26.6 us (4%)
    ppermute x30, starting transfers between devices, shifted(): lax.ppermute(value, axis, [(source, source + steps) for source in range(l...  204 us
    ppermute x30, waiting for transfers between devices, shifted(): lax.ppermute(value, axis, [(source, source + steps) for source in range(l...  188 us
    dot_general x8, matrix products, turn(): jnp.einsum('hrw,rhd->whd', probs_b, grad_cols, preferred_element_type=jnp...  29.7 us
    dot_general x8, matrix products, turn(): jnp.einsum('hrw,whd->rhd', probs_b, value_cols, preferred_element_type=jn...  28.7 us
    cond x2, local copies, waits for them, and re-layouts, shards(): result = lax.cond(far_needed, attend_full, attend_near)  24.2 us
    sub x8, matrix products, turn(): weights = jnp.exp(scores - peak)  21.3 us
    unnamed x29, local copies, waits for them, and re-layouts  20.1 us
    dot_general x8, matrix products, turn(): jnp.einsum('rhd,whd->hrw', grad_cols, value_cols, preferred_element_type=...  14.3 us
  transfers between devices with their start and end apart: 30, of which 13 were waited for; matrix products, arithmetic and copies ran while one was open for 7% of the time, Pallas kernels for 0%

commit v1 on v0

v1 whole, which is shorter than its diff:
```python
import math

import jax
import jax.numpy as jnp
from jax import lax
from jax.experimental import pallas as pl
from jax.experimental.pallas import tpu as pltpu
from jax.sharding import PartitionSpec as P

D = 1024
HEADS = 16
HEAD_DIM = 64
ROWS = 384
MOST = 1152
N_IMG = 128
GROUP = 8
GROUPS = N_IMG // GROUP
GROUP_ROWS = GROUP * ROWS
REACH = 3
LANES = 128
EXT_ROWS = GROUP_ROWS + 2 * MOST
K_STEP = 256
PAD_ROWS = EXT_ROWS + K_STEP
TILES = GROUP_ROWS // LANES
TAG_ROWS = 16
MAX_STEPS = 11
SCALE = 1.0 / math.sqrt(HEAD_DIM)
EXP_SCALE = SCALE * math.log2(math.e)
NEG = -1e30


def group_lists():
    return [[g * GROUP + i for i in range(GROUP)] for g in range(GROUPS)]


def shifted(value, steps):
    leading, last = max(0, -steps), min(N_IMG, N_IMG - steps)
    return lax.ppermute(value, "img", [(s, s + steps) for s in range(leading, last)])


def dot_nt(a, b):
    return lax.dot_general(a, b, (((1,), (1,)), ((), ())), preferred_element_type=jnp.float32)


def dot_nn(a, b):
    return lax.dot_general(a, b, (((1,), (0,)), ((), ())), preferred_element_type=jnp.float32)


def fold_rows(x):
    return x.reshape(x.shape[0] // 8, 8, x.shape[1])


def attend_kernel(
    lo_ref, hi_ref, start_ref, end_ref, own_ref, left_ref, right_ref, qg_ref,
    oq_ref, own_kv_ref, left_kv_ref, right_kv_ref,
    kx, vx, kt, vt, dk, dv, sbuf, dbuf, ot, qt,
):
    for j in range(REACH):
        a = j * ROWS
        b = MOST + GROUP_ROWS + j * ROWS
        kx[a : a + ROWS, :] = left_ref[j, 0:ROWS, :]
        vx[a : a + ROWS, :] = left_ref[j, ROWS : 2 * ROWS, :]
        kx[b : b + ROWS, :] = right_ref[j, 0:ROWS, :]
        vx[b : b + ROWS, :] = right_ref[j, ROWS : 2 * ROWS, :]
    for j in range(GROUP):
        a = MOST + j * ROWS
        kx[a : a + ROWS, :] = own_ref[j, 0:ROWS, :]
        vx[a : a + ROWS, :] = own_ref[j, ROWS : 2 * ROWS, :]
    kx[EXT_ROWS:PAD_ROWS, :] = jnp.zeros((PAD_ROWS - EXT_ROWS, LANES), jnp.bfloat16)
    vx[EXT_ROWS:PAD_ROWS, :] = jnp.zeros((PAD_ROWS - EXT_ROWS, LANES), jnp.bfloat16)
    dk[...] = jnp.zeros_like(dk)
    dv[...] = jnp.zeros_like(dv)

    def transpose_chunk(c, _):
        at = pl.multiple_of(c * LANES, LANES)
        kt[:, pl.ds(at, LANES)] = kx[pl.ds(at, LANES), :].T
        vt[:, pl.ds(at, LANES)] = vx[pl.ds(at, LANES), :].T
        return 0

    lax.fori_loop(0, PAD_ROWS // LANES, transpose_chunk, 0)

    lane = lax.broadcasted_iota(jnp.int32, (LANES, LANES), 1)
    first_head = lane < HEAD_DIM
    row_index = lax.broadcasted_iota(jnp.int32, (K_STEP, 2 * LANES), 0)

    def q_tile(t, _):
        dev = t // REACH
        off = pl.multiple_of((t % REACH) * LANES, LANES)
        q = qg_ref[dev, pl.ds(off, LANES), :]
        g = qg_ref[dev, pl.ds(off + ROWS, LANES), :]
        zero = jnp.zeros_like(q)
        q2 = jnp.concatenate([jnp.where(first_head, q, zero), jnp.where(first_head, zero, q)], 0)
        g2 = jnp.concatenate([jnp.where(first_head, g, zero), jnp.where(first_head, zero, g)], 0)
        begin = start_ref[pl.ds(t, 1), :]
        stop = end_ref[pl.ds(t, 1), :]
        begin = jnp.concatenate([begin, begin], 1)
        stop = jnp.concatenate([stop, stop], 1)
        k0 = (lo_ref[t] // LANES) * LANES
        steps = (hi_ref[t] - k0 + K_STEP - 1) // K_STEP

        def scores(i, top):
            at = pl.multiple_of(k0 + i * K_STEP, LANES)
            s = dot_nt(kx[pl.ds(at, K_STEP), :], q2)
            index = row_index + at
            s = jnp.where((index >= begin) & (index < stop), s, NEG)
            sbuf[pl.ds(pl.multiple_of(i * K_STEP, K_STEP), K_STEP), :] = s
            return jnp.maximum(top, jnp.max(fold_rows(s), axis=0))

        top = lax.fori_loop(0, steps, scores, jnp.full((8, 2 * LANES), NEG, jnp.float32))
        top = jnp.max(top, axis=0, keepdims=True)

        def weigh(i, carry):
            total, delta = carry
            at = pl.multiple_of(k0 + i * K_STEP, LANES)
            here = pl.ds(pl.multiple_of(i * K_STEP, K_STEP), K_STEP)
            e = jnp.exp2((sbuf[here, :] - top) * EXP_SCALE)
            d = dot_nt(vx[pl.ds(at, K_STEP), :], g2)
            sbuf[here, :] = e
            dbuf[here, :] = d
            total = total + jnp.sum(fold_rows(e), axis=0)
            delta = delta + jnp.sum(fold_rows(e * d), axis=0)
            return total, delta

        zeros8 = jnp.zeros((8, 2 * LANES), jnp.float32)
        total, delta = lax.fori_loop(0, steps, weigh, (zeros8, zeros8))
        inverse = 1.0 / jnp.sum(total, axis=0, keepdims=True)
        delta = jnp.sum(delta, axis=0, keepdims=True) * inverse
        ot[...] = jnp.zeros_like(ot)
        qt[...] = jnp.zeros_like(qt)

        def spread(i, _):
            at = pl.multiple_of(k0 + i * K_STEP, LANES)
            here = pl.ds(pl.multiple_of(i * K_STEP, K_STEP), K_STEP)
            rows = pl.ds(at, K_STEP)
            p = sbuf[here, :] * inverse
            ds = (p * (dbuf[here, :] - delta)).astype(jnp.bfloat16)
            p = p.astype(jnp.bfloat16)
            dv[rows, :] += dot_nn(p, g2)
            dk[rows, :] += dot_nn(ds, q2)
            ot[...] += dot_nn(vt[:, rows], p)
            qt[...] += dot_nn(kt[:, rows], ds)
            return 0

        lax.fori_loop(0, steps, spread, 0)
        o = jnp.concatenate([ot[0:HEAD_DIM, 0:LANES], ot[HEAD_DIM:LANES, LANES : 2 * LANES]], 0)
        dq = jnp.concatenate([qt[0:HEAD_DIM, 0:LANES], qt[HEAD_DIM:LANES, LANES : 2 * LANES]], 0)
        oq_ref[dev, pl.ds(off, LANES), :] = o.T.astype(jnp.bfloat16)
        oq_ref[dev, pl.ds(off + ROWS, LANES), :] = (dq.T * SCALE).astype(jnp.bfloat16)
        return 0

    lax.fori_loop(0, TILES, q_tile, 0)
    left_kv_ref[0] = (dk[0:MOST, :] * SCALE).astype(jnp.bfloat16)
    left_kv_ref[1] = dv[0:MOST, :].astype(jnp.bfloat16)
    right_kv_ref[0] = (dk[MOST + GROUP_ROWS : EXT_ROWS, :] * SCALE).astype(jnp.bfloat16)
    right_kv_ref[1] = dv[MOST + GROUP_ROWS : EXT_ROWS, :].astype(jnp.bfloat16)
    own_kv_ref[0] = dk[MOST : MOST + GROUP_ROWS, :] * SCALE
    own_kv_ref[1] = dv[MOST : MOST + GROUP_ROWS, :]


def attend(lo, hi, start, end, own, left, right, qg):
    smem = pl.BlockSpec(memory_space=pltpu.SMEM)
    vmem = pl.BlockSpec(memory_space=pltpu.VMEM)
    bf16, f32 = jnp.bfloat16, jnp.float32
    return pl.pallas_call(
        attend_kernel,
        out_shape=(
            jax.ShapeDtypeStruct((GROUP, 2 * ROWS, LANES), bf16),
            jax.ShapeDtypeStruct((2, GROUP_ROWS, LANES), f32),
            jax.ShapeDtypeStruct((2, MOST, LANES), bf16),
            jax.ShapeDtypeStruct((2, MOST, LANES), bf16),
        ),
        in_specs=[smem, smem] + [vmem] * 6,
        out_specs=(vmem,) * 4,
        scratch_shapes=[
            pltpu.VMEM((PAD_ROWS, LANES), bf16),
            pltpu.VMEM((PAD_ROWS, LANES), bf16),
            pltpu.VMEM((LANES, PAD_ROWS), bf16),
            pltpu.VMEM((LANES, PAD_ROWS), bf16),
            pltpu.VMEM((PAD_ROWS, LANES), f32),
            pltpu.VMEM((PAD_ROWS, LANES), f32),
            pltpu.VMEM((MAX_STEPS * K_STEP, 2 * LANES), f32),
            pltpu.VMEM((MAX_STEPS * K_STEP, 2 * LANES), f32),
            pltpu.VMEM((LANES, 2 * LANES), f32),
            pltpu.VMEM((LANES, 2 * LANES), f32),
        ],
        compiler_params=pltpu.CompilerParams(vmem_limit_bytes=48 * 1024 * 1024),
        cost_estimate=pl.CostEstimate(
            flops=20_000_000_000, bytes_accessed=12_000_000, transcendentals=6_000_000
        ),
        name="attend",
    )(lo, hi, start, end, own, left, right, qg)


def split_heads(x):
    return x.reshape(ROWS, GROUP, LANES).transpose(1, 0, 2)


def exchange(x):
    return lax.all_to_all(x, "img", 0, 0, axis_index_groups=group_lists())


def merge_heads(x):
    return x.transpose(1, 0, 2).reshape(ROWS, D)


def shards(queries, keys, values, out_grad, image_ids):
    tags = (image_ids + 1).astype(jnp.bfloat16).reshape(ROWS // LANES, LANES)
    tags = jnp.pad(tags, ((0, TAG_ROWS - ROWS // LANES), (0, 0)))
    tags = jnp.broadcast_to(tags[None], (GROUP, TAG_ROWS, LANES))
    own = exchange(jnp.concatenate([split_heads(keys), split_heads(values), tags], 1))
    left = shifted(own[GROUP - REACH :], GROUP)
    right = shifted(own[:REACH], -GROUP)
    qg = exchange(jnp.concatenate([split_heads(queries), split_heads(out_grad)], 1))

    def tags_of(x):
        return x[:, 2 * ROWS : 2 * ROWS + ROWS // LANES, :].astype(jnp.int32).reshape(-1)

    own_tags = tags_of(own)
    right_tags = tags_of(right)
    is_last = lax.axis_index("img") >= N_IMG - GROUP
    right_tags = jnp.where(is_last, N_IMG + 1, right_tags)
    ext_tags = jnp.concatenate([tags_of(left), own_tags, right_tags])
    every = jnp.arange(N_IMG + 1, dtype=jnp.int32)
    below = jnp.sum((ext_tags[None, :] < every[:, None]).astype(jnp.int32), 1)
    upto = jnp.sum((ext_tags[None, :] <= every[:, None]).astype(jnp.int32), 1)
    pick = own_tags[:, None] == every[None, :]
    start = jnp.sum(jnp.where(pick, below[None, :], 0), 1).reshape(TILES, LANES)
    end = jnp.sum(jnp.where(pick, upto[None, :], 0), 1).reshape(TILES, LANES)
    oq, own_kv, left_kv, right_kv = attend(
        start[:, 0], end[:, LANES - 1], start, end, own, left, right, qg
    )
    from_next = shifted(left_kv, -GROUP)
    from_prev = shifted(right_kv, GROUP)
    oq = exchange(oq)
    kv = own_kv.at[:, GROUP_ROWS - MOST :].add(from_next.astype(jnp.float32))
    kv = kv.at[:, :MOST].add(from_prev.astype(jnp.float32))
    kv = kv.astype(jnp.bfloat16).reshape(2, GROUP, ROWS, LANES).transpose(1, 0, 2, 3)
    kv = exchange(kv.reshape(GROUP, 2 * ROWS, LANES))
    return (
        merge_heads(oq[:, :ROWS]),
        merge_heads(oq[:, ROWS:]),
        merge_heads(kv[:, :ROWS]),
        merge_heads(kv[:, ROWS:]),
    )


def solution(mesh):
    in_specs = (P("img", None), P("img", None), P("img", None), P("img", None), P("img"))
    out_specs = (P("img", None), P("img", None), P("img", None), P("img", None))
    return jax.shard_map(shards, mesh=mesh, in_specs=in_specs, out_specs=out_specs, check_vma=False)
```

time: 680 us -> 217 us (0.32)
  the two profiles are of different devices: /device:TPU:124 before, /device:TPU:2 now
where the time goes in v1:
time: 217 us; the launch traced here: 218 us
  Pallas kernels  87.3 us (40%)
  waiting for transfers between devices  48.6 us (22%)
  blocking collectives  26.4 us (12%)
  starting transfers between devices  25.6 us (12%)
  local copies, waits for them, and re-layouts  17.9 us (8%)
  other arithmetic  11.1 us (5%)
    pallas_call x1, Pallas kernels, attend(): pl.pallas_call(attend_kernel, out_shape=(jax.ShapeDtypeStruct((GROUP, 2 *...  87.3 us
    all_to_all x3, waiting for transfers between devices, exchange(): return lax.all_to_all(x, 'img', 0, 0, axis_index_groups=group_lists())  27.6 us
    all_to_all x1, blocking collectives, exchange(): return lax.all_to_all(x, 'img', 0, 0, axis_index_groups=group_lists())  26.4 us
    ppermute x4, waiting for transfers between devices, shifted(): lax.ppermute(value, 'img', [(s, s + steps) for s in range(leading, last)])  21 us
    ppermute x4, starting transfers between devices, shifted(): lax.ppermute(value, 'img', [(s, s + steps) for s in range(leading, last)])  13.9 us
    all_to_all x3, starting transfers between devices, exchange(): return lax.all_to_all(x, 'img', 0, 0, axis_index_groups=group_lists())  11.6 us
    unnamed x18, local copies, waits for them, and re-layouts  7.73 us
    transpose x6, local copies, waits for them, and re-layouts, merge_heads(): return x.transpose(1, 0, 2).reshape(ROWS, D)  6.02 us
  transfers between devices with their start and end apart: 7, of which 6 were waited for; matrix products, arithmetic and copies ran while one was open for 9% of the time, Pallas kernels for 0%

profile of v1, /device:TPU:2, one launch (start us, length us, event | category | flops | bytes accessed | tf_op | source)
XLA Modules:
  0.0 217.6 jit_solution(11991187173666686362)
XLA Ops:
  1.4 1.5 copy.39
  4.2 26.4 %all_to_all.20.own_ref = bf16[8,784,128]{2,1,0:T(8,128)(2,1)S(1)} all-to-all(bf16[8,784,128]{2,1,0:T(8,128)(2,1)S(1)} %pad_maximum_fusion), channel_id=1, replica_groups={{0,1,2,3,4,5,6,7},{8,9,10,11,12,13,14,15},{16,17,18,19,20,21,22,23},{24..., dimensions={0} | all-to-all | bytes 3211264 | tf_op jit(solution)/shard_map/all_to_all | solution.py:199
  32.2 3.9 %collective-permute-start = (bf16[3,784,128]{2,1,0:T(8,128)(2,1)}, bf16[3,784,128]{2,1,0:T(8,128)(2,1)S(1)}, u32[]{:S(2)}, u32[]{:S(2)}) collective-permute-start(bf16[3,784,128]{2,1,0:T(8,128)(2,1)} %get-tuple-element.52), channel_id=1, source_target_pairs={{0,8},{1,9},{2,10},{3,11},{4,12},{5,13},{6,14},{7,15},{8,16},{9,17... | collective-permute-start | bytes 1806344 | tf_op jit(solution)/shard_map/ppermute | solution.py:38
  37.7 4.1 %collective-permute-start.1 = (bf16[3,784,128]{2,1,0:T(8,128)(2,1)}, bf16[3,784,128]{2,1,0:T(8,128)(2,1)S(1)}, u32[]{:S(2)}, u32[]{:S(2)}) collective-permute-start(bf16[3,784,128]{2,1,0:T(8,128)(2,1)} %get-tuple-element.53), channel_id=1, source_target_pairs={{8,0},{9,1},{10,2},{11,3},{12,4},{13,5},{14,6},{15,7},{16,8},{17,9... | collective-permute-start | bytes 1806344 | tf_op jit(solution)/shard_map/ppermute | solution.py:38
  41.8 1.3 pad_maximum_fusion.1
  43.1 3.6 %all-to-all-start.1 = ((bf16[8,768,128]{2,1,0:T(8,128)(2,1)}), bf16[8,768,128]{2,1,0:T(8,128)(2,1)S(1)}, u32[]{:S(2)}, u32[]{:S(2)}) async-start(bf16[8,768,128]{2,1,0:T(8,128)(2,1)} %pad_maximum_fusion.1), calls=%async_computation.1 | async-start | bytes 3145728 | tf_op jit(solution)/shard_map/all_to_all | solution.py:199
  47.4 4.7 %collective-permute-done.left_ref = bf16[3,784,128]{2,1,0:T(8,128)(2,1)S(1)} collective-permute-done((bf16[3,784,128]{2,1,0:T(8,128)(2,1)}, bf16[3,784,128]{2,1,0:T(8,128)(2,1)S(1)}, u32[]{:S(2)}, u32[]{:S(2)}) %collective-permute-start) | collective-permute-done | bytes 602144 | tf_op jit(solution)/shard_map/ppermute | solution.py:38
  52.1 3.0 %collective-permute-done.1.right_ref = bf16[3,784,128]{2,1,0:T(8,128)(2,1)S(1)} collective-permute-done((bf16[3,784,128]{2,1,0:T(8,128)(2,1)}, bf16[3,784,128]{2,1,0:T(8,128)(2,1)S(1)}, u32[]{:S(2)}, u32[]{:S(2)}) %collective-permute-start.1) | collective-permute-done | bytes 602144 | tf_op jit(solution)/shard_map/ppermute | solution.py:38
  56.6 11.6 %all-to-all-done.1.qg_ref = bf16[8,768,128]{2,1,0:T(8,128)(2,1)S(1)} async-done(((bf16[8,768,128]{2,1,0:T(8,128)(2,1)}), bf16[8,768,128]{2,1,0:T(8,128)(2,1)S(1)}, u32[]{:S(2)}, u32[]{:S(2)}) %all-to-all-start.1) | async-done | bytes 1572896 | tf_op jit(solution)/shard_map/all_to_all | solution.py:199
  68.2 87.3 %attend.1 = (bf16[8,768,128]{2,1,0:T(8,128)(2,1)}, f32[2,3072,128]{2,1,0:T(8,128)}, bf16[2,1152,128]{2,1,0:T(8,128)(2,1)}, bf16[2,1152,128]{2,1,0:T(8,128)(2,1)S(1)}) custom-call(s32[24]{0:T(128)S(1)} %get-tuple-element.59.lo_ref, s32[24]{0:T(128)S(1)} %get-tuple-element.58.hi_ref, s32[24,128]{1,0:T(8,128)S(1)} %bitcast.31, s32[24,128]{1,0:T(8,128)S(1)} %bitcast.29, ...), custom_call_target="tpu_custom_call" | custom-call | flops 20000000000 | bytes 12000000 | tf_op jit(solution)/shard_map/attend/pallas_call | solution.py:164
  155.4 1.9 collective-permute-start.2
  157.3 3.6 %all-to-all-start.2 = ((bf16[8,768,128]{2,1,0:T(8,128)(2,1)}), bf16[8,768,128]{2,1,0:T(8,128)(2,1)S(1)}, u32[]{:S(2)}, u32[]{:S(2)}) async-start(bf16[8,768,128]{2,1,0:T(8,128)(2,1)} %get-tuple-element.32), calls=%async_computation.2 | async-start | bytes 3145728 | tf_op jit(solution)/shard_map/all_to_all | solution.py:199
  160.9 4.0 %collective-permute-start.3 = (bf16[2,1152,128]{2,1,0:T(8,128)(2,1)S(1)}, bf16[2,1152,128]{2,1,0:T(8,128)(2,1)S(1)}, u32[]{:S(2)}, u32[]{:S(2)}) collective-permute-start(bf16[2,1152,128]{2,1,0:T(8,128)(2,1)S(1)} %get-tuple-element.35), channel_id=1, source_target_pairs={{0,8},{1,9},{2,10},{3,11},{4,12},{5,13},{6,14},{7,15},{8,16},{9,17... | collective-permute-start | bytes 1769480 | tf_op jit(solution)/shard_map/ppermute | solution.py:38
  164.9 7.5 %collective-permute-done.2 = bf16[2,1152,128]{2,1,0:T(8,128)(2,1)S(1)} collective-permute-done((bf16[2,1152,128]{2,1,0:T(8,128)(2,1)}, bf16[2,1152,128]{2,1,0:T(8,128)(2,1)S(1)}, u32[]{:S(2)}, u32[]{:S(2)}) %collective-permute-start.2) | collective-permute-done | bytes 589856 | tf_op jit(solution)/shard_map/ppermute | solution.py:38
  172.4 2.4 %add_dynamic-update-slice_fusion = f32[2,3072,128]{2,1,0:T(8,128)} fusion(f32[2,3072,128]{2,1,0:T(8,128)} %get-tuple-element.33, bf16[2,1152,128]{2,1,0:T(8,128)(2,1)S(1)} %collective-permute-done.2), kind=kLoop, calls=%fused_computation.11 | loop fusion | flops 589824 | bytes 2949120 | tf_op jit(solution)/shard_map/scatter-add | solution.py:235
  174.8 5.8 %collective-permute-done.3 = bf16[2,1152,128]{2,1,0:T(8,128)(2,1)S(1)} collective-permute-done((bf16[2,1152,128]{2,1,0:T(8,128)(2,1)S(1)}, bf16[2,1152,128]{2,1,0:T(8,128)(2,1)S(1)}, u32[]{:S(2)}, u32[]{:S(2)}) %collective-permute-start.3) | collective-permute-done | bytes 589856 | tf_op jit(solution)/shard_map/ppermute | solution.py:38
  180.6 2.4 %fusion = f32[2,3072,128]{2,1,0:T(8,128)} fusion(f32[2,3072,128]{2,1,0:T(8,128)} %add_dynamic-update-slice_fusion, bf16[2,1152,128]{2,1,0:T(8,128)(2,1)S(1)} %collective-permute-done.3), kind=kLoop, calls=%fused_computation.10 | loop fusion | flops 589824 | bytes 2949120 | tf_op jit(solution)/shard_map/scatter-add | solution.py:236
  183.0 2.1 convert_element_type.31
  185.1 1.3 copy.49
  186.3 4.5 %all-to-all-start.3 = ((bf16[8,768,128]{2,1,0:T(8,128)(2,1)}), bf16[8,768,128]{2,1,0:T(8,128)(2,1)S(1)}, u32[]{:S(2)}, u32[]{:S(2)}) async-start(bf16[8,768,128]{2,1,0:T(8,128)(2,1)} %bitcast.32), calls=%async_computation.3 | async-start | bytes 3145728 | tf_op jit(solution)/shard_map/all_to_all | solution.py:199
  190.8 1.2 slice_bitcast_fusion.2
  192.1 1.6 copy.48
  196.3 16.1 %all-to-all-done.3 = bf16[8,768,128]{2,1,0:T(8,128)(2,1)S(1)} async-done(((bf16[8,768,128]{2,1,0:T(8,128)(2,1)}), bf16[8,768,128]{2,1,0:T(8,128)(2,1)S(1)}, u32[]{:S(2)}, u32[]{:S(2)}) %all-to-all-start.3) | async-done | bytes 1572896 | tf_op jit(solution)/shard_map/all_to_all | solution.py:199
  213.4 1.5 copy.51
  (40 shorter events, 13.7 us)
Async XLA Ops:
  0.6 2.6 %copy-start.2 = (bf16[384,1024]{1,0:T(8,128)(2,1)S(1)}, bf16[384,1024]{1,0:T(8,128)(2,1)}, u32[]{:S(2)}) copy-start(bf16[384,1024]{1,0:T(8,128)(2,1)} %param.11) | copy-start | bytes 2359300
  30.6 1.6 copy-start
  30.6 5.5 %copy-start.3 = (bf16[384,1024]{1,0:T(8,128)(2,1)S(1)}, bf16[384,1024]{1,0:T(8,128)(2,1)}, u32[]{:S(2)}) copy-start(bf16[384,1024]{1,0:T(8,128)(2,1)} %param.9) | copy-start | bytes 2359300
  32.2 4.7 %copy-start.4 = (bf16[384,1024]{1,0:T(8,128)(2,1)S(1)}, bf16[384,1024]{1,0:T(8,128)(2,1)}, u32[]{:S(2)}) copy-start(bf16[384,1024]{1,0:T(8,128)(2,1)} %param.12) | copy-start | bytes 2359300
  32.2 19.9 %collective-permute-start = (bf16[3,784,128]{2,1,0:T(8,128)(2,1)}, bf16[3,784,128]{2,1,0:T(8,128)(2,1)S(1)}, u32[]{:S(2)}, u32[]{:S(2)}) collective-permute-start(bf16[3,784,128]{2,1,0:T(8,128)(2,1)} %get-tuple-element.52), channel_id=1, source_target_pairs={{0,8},{1,9},{2,10},{3,11},{4,12},{5,13},{6,14},{7,15},{8,16},{9,17... | collective-permute-start | bytes 1806344 | tf_op jit(solution)/shard_map/ppermute | solution.py:38
  37.7 17.4 %collective-permute-start.1 = (bf16[3,784,128]{2,1,0:T(8,128)(2,1)}, bf16[3,784,128]{2,1,0:T(8,128)(2,1)S(1)}, u32[]{:S(2)}, u32[]{:S(2)}) collective-permute-start(bf16[3,784,128]{2,1,0:T(8,128)(2,1)} %get-tuple-element.53), channel_id=1, source_target_pairs={{8,0},{9,1},{10,2},{11,3},{12,4},{13,5},{14,6},{15,7},{16,8},{17,9... | collective-permute-start | bytes 1806344 | tf_op jit(solution)/shard_map/ppermute | solution.py:38
  43.1 25.1 %all-to-all-start.1 = ((bf16[8,768,128]{2,1,0:T(8,128)(2,1)}), bf16[8,768,128]{2,1,0:T(8,128)(2,1)S(1)}, u32[]{:S(2)}, u32[]{:S(2)}) async-start(bf16[8,768,128]{2,1,0:T(8,128)(2,1)} %pad_maximum_fusion.1), calls=%async_computation.1 | async-start | bytes 3145728 | tf_op jit(solution)/shard_map/all_to_all | solution.py:199
  155.4 17.0 %collective-permute-start.2 = (bf16[2,1152,128]{2,1,0:T(8,128)(2,1)}, bf16[2,1152,128]{2,1,0:T(8,128)(2,1)S(1)}, u32[]{:S(2)}, u32[]{:S(2)}) collective-permute-start(bf16[2,1152,128]{2,1,0:T(8,128)(2,1)} %get-tuple-element.34), channel_id=1, source_target_pairs={{8,0},{9,1},{10,2},{11,3},{12,4},{13,5},{14,6},{15,7},{16,8},{17,9... | collective-permute-start | bytes 1769480 | tf_op jit(solution)/shard_map/ppermute | solution.py:38
  157.3 29.0 %all-to-all-start.2 = ((bf16[8,768,128]{2,1,0:T(8,128)(2,1)}), bf16[8,768,128]{2,1,0:T(8,128)(2,1)S(1)}, u32[]{:S(2)}, u32[]{:S(2)}) async-start(bf16[8,768,128]{2,1,0:T(8,128)(2,1)} %get-tuple-element.32), calls=%async_computation.2 | async-start | bytes 3145728 | tf_op jit(solution)/shard_map/all_to_all | solution.py:199
  160.9 19.6 %collective-permute-start.3 = (bf16[2,1152,128]{2,1,0:T(8,128)(2,1)S(1)}, bf16[2,1152,128]{2,1,0:T(8,128)(2,1)S(1)}, u32[]{:S(2)}, u32[]{:S(2)}) collective-permute-start(bf16[2,1152,128]{2,1,0:T(8,128)(2,1)S(1)} %get-tuple-element.35), channel_id=1, source_target_pairs={{0,8},{1,9},{2,10},{3,11},{4,12},{5,13},{6,14},{7,15},{8,16},{9,17... | collective-permute-start | bytes 1769480 | tf_op jit(solution)/shard_map/ppermute | solution.py:38
  186.3 26.1 %all-to-all-start.3 = ((bf16[8,768,128]{2,1,0:T(8,128)(2,1)}), bf16[8,768,128]{2,1,0:T(8,128)(2,1)S(1)}, u32[]{:S(2)}, u32[]{:S(2)}) async-start(bf16[8,768,128]{2,1,0:T(8,128)(2,1)} %bitcast.32), calls=%async_computation.3 | async-start | bytes 3145728 | tf_op jit(solution)/shard_map/all_to_all | solution.py:199
  192.1 2.7 %copy-start.1 = (bf16[384,8,128]{2,0,1:T(8,128)(2,1)S(1)}, bf16[384,8,128]{2,0,1:T(8,128)(2,1)}, u32[]{:S(2)}) copy-start(bf16[384,8,128]{2,0,1:T(8,128)(2,1)} %get-tuple-element.57) | copy-start | bytes 2359300

commit v2 on v1

v2 whole, which is shorter than its diff:
```python
import math

import jax
import jax.numpy as jnp
from jax import lax
from jax.experimental import pallas as pl
from jax.experimental.pallas import tpu as pltpu
from jax.sharding import PartitionSpec as P

D = 1024
HEAD_DIM = 64
ROWS = 384
MOST = 1152
N_IMG = 128
GROUP = 8
GROUPS = N_IMG // GROUP
GROUP_ROWS = GROUP * ROWS
REACH = 3
LANES = 128
EXT_ROWS = GROUP_ROWS + 2 * MOST
K_STEP = 256
PAD_ROWS = EXT_ROWS + K_STEP
TILES = GROUP_ROWS // LANES
TAG_ROWS = 16
MAX_STEPS = 11
UNROLLED = 8
PAIR = 2
SCALE = 1.0 / math.sqrt(HEAD_DIM)
EXP_SCALE = SCALE * math.log2(math.e)
NEG = -1e30


def group_lists():
    return [[g * GROUP + i for i in range(GROUP)] for g in range(GROUPS)]


def shifted(value, steps):
    leading, last = max(0, -steps), min(N_IMG, N_IMG - steps)
    return lax.ppermute(value, "img", [(s, s + steps) for s in range(leading, last)])


def dot_nt(a, b):
    return lax.dot_general(a, b, (((1,), (1,)), ((), ())), preferred_element_type=jnp.float32)


def dot_nn(a, b):
    return lax.dot_general(a, b, (((1,), (0,)), ((), ())), preferred_element_type=jnp.float32)


def fold_rows(x):
    return x.reshape(x.shape[0] // 8, 8, x.shape[1])


def attend_kernel(
    lo_ref, hi_ref, start_ref, end_ref, own_ref, left_ref, right_ref, qg_ref,
    oq_ref, own_kv_ref, left_kv_ref, right_kv_ref,
    kx, vx, kt, vt, dk, dv, sbuf, dbuf, ot, qt,
):
    for j in range(REACH):
        a = j * ROWS
        b = MOST + GROUP_ROWS + j * ROWS
        kx[a : a + ROWS, :] = left_ref[j, 0:ROWS, :]
        vx[a : a + ROWS, :] = left_ref[j, ROWS : 2 * ROWS, :]
        kx[b : b + ROWS, :] = right_ref[j, 0:ROWS, :]
        vx[b : b + ROWS, :] = right_ref[j, ROWS : 2 * ROWS, :]
    for j in range(GROUP):
        a = MOST + j * ROWS
        kx[a : a + ROWS, :] = own_ref[j, 0:ROWS, :]
        vx[a : a + ROWS, :] = own_ref[j, ROWS : 2 * ROWS, :]
    kx[EXT_ROWS:PAD_ROWS, :] = jnp.zeros((PAD_ROWS - EXT_ROWS, LANES), jnp.bfloat16)
    vx[EXT_ROWS:PAD_ROWS, :] = jnp.zeros((PAD_ROWS - EXT_ROWS, LANES), jnp.bfloat16)
    dk[...] = jnp.zeros_like(dk)
    dv[...] = jnp.zeros_like(dv)

    def transpose_chunk(c, _):
        at = pl.multiple_of(c * K_STEP, K_STEP)
        kt[:, pl.ds(at, K_STEP)] = kx[pl.ds(at, K_STEP), :].T
        vt[:, pl.ds(at, K_STEP)] = vx[pl.ds(at, K_STEP), :].T
        return 0

    lax.fori_loop(0, PAD_ROWS // K_STEP, transpose_chunk, 0)

    lane = lax.broadcasted_iota(jnp.int32, (LANES, LANES), 1)
    first_head = lane < HEAD_DIM
    row_index = lax.broadcasted_iota(jnp.int32, (K_STEP, LANES), 0)

    def both_heads(x):
        zero = jnp.zeros_like(x)
        return jnp.concatenate([jnp.where(first_head, x, zero), jnp.where(first_head, zero, x)], 0)

    def step_count(t):
        return (hi_ref[t] - (lo_ref[t] // LANES) * LANES + K_STEP - 1) // K_STEP

    def q_tiles(u, _):
        tiles = [u * PAIR + j for j in range(PAIR)]
        steps = step_count(tiles[0])
        for t in tiles[1:]:
            steps = jnp.maximum(steps, step_count(t))
        subs = []
        for j, t in enumerate(tiles):
            dev = t // REACH
            off = pl.multiple_of((t % REACH) * LANES, LANES)
            k0 = jnp.minimum((lo_ref[t] // LANES) * LANES, PAD_ROWS - steps * K_STEP)
            subs.append((j, t, dev, off, k0))

        def tile_part(sub, run):
            j, t, dev, off, k0 = sub
            q2 = both_heads(qg_ref[dev, pl.ds(off, LANES), :])
            g2 = both_heads(qg_ref[dev, pl.ds(off + ROWS, LANES), :])
            begin = start_ref[pl.ds(t, 1), :]
            stop = end_ref[pl.ds(t, 1), :]

            def rows_at(i):
                return pl.ds(pl.multiple_of(k0 + i * K_STEP, LANES), K_STEP)

            def here_at(i):
                return pl.ds(i * K_STEP if isinstance(i, int) else pl.multiple_of(i * K_STEP, K_STEP), K_STEP)

            def scores(i, top):
                s = dot_nt(kx[rows_at(i), :], q2)
                index = row_index + (k0 + i * K_STEP)
                keep = (index >= begin) & (index < stop)
                s = jnp.where(jnp.concatenate([keep, keep], 1), s, NEG)
                sbuf[j, here_at(i), :] = s
                dbuf[j, here_at(i), :] = dot_nt(vx[rows_at(i), :], g2)
                return jnp.maximum(top, jnp.max(fold_rows(s), axis=0))

            def weigh(i, carry):
                top, total, delta = carry
                e = jnp.exp2((sbuf[j, here_at(i), :] - top) * EXP_SCALE)
                sbuf[j, here_at(i), :] = e
                total = total + jnp.sum(fold_rows(e), axis=0)
                delta = delta + jnp.sum(fold_rows(e * dbuf[j, here_at(i), :]), axis=0)
                return top, total, delta

            def spread(i, carry):
                inverse, delta = carry
                rows = rows_at(i)
                p = sbuf[j, here_at(i), :] * inverse
                ds = (p * (dbuf[j, here_at(i), :] - delta)).astype(jnp.bfloat16)
                p = p.astype(jnp.bfloat16)
                dv[rows, :] += dot_nn(p, g2)
                dk[rows, :] += dot_nn(ds, q2)
                o = dot_nn(vt[:, rows], p)
                dq = dot_nn(kt[:, rows], ds)
                parts = ((o, ot), (dq, qt))
                for value, ref in parts:
                    top_part = value[0:HEAD_DIM, 0:LANES]
                    low_part = value[HEAD_DIM:LANES, LANES : 2 * LANES]
                    if isinstance(i, int) and i == 0:
                        ref[j, 0:HEAD_DIM, :] = top_part
                        ref[j, HEAD_DIM:LANES, :] = low_part
                    else:
                        ref[j, 0:HEAD_DIM, :] += top_part
                        ref[j, HEAD_DIM:LANES, :] += low_part
                return carry

            def first():
                top = run(scores, jnp.full((8, 2 * LANES), NEG, jnp.float32))
                return jnp.max(top, axis=0, keepdims=True)

            def second(top):
                zeros8 = jnp.zeros((8, 2 * LANES), jnp.float32)
                _, total, delta = run(weigh, (top, zeros8, zeros8))
                inverse = 1.0 / jnp.sum(total, axis=0, keepdims=True)
                return inverse, jnp.sum(delta, axis=0, keepdims=True) * inverse

            def third(carry):
                run(spread, carry)
                oq_ref[dev, pl.ds(off, LANES), :] = ot[j].T.astype(jnp.bfloat16)
                oq_ref[dev, pl.ds(off + ROWS, LANES), :] = (qt[j].T * SCALE).astype(jnp.bfloat16)

            return first, second, third

        def whole(run):
            parts = [tile_part(sub, run) for sub in subs]
            tops = [p[0]() for p in parts]
            stats = [p[1](top) for p, top in zip(parts, tops)]
            for p, stat in zip(parts, stats):
                p[2](stat)

        def unrolled(count):
            def run(body, carry):
                for i in range(count):
                    carry = body(i, carry)
                return carry

            return lambda: whole(run)

        def looped():
            ot[...] = jnp.zeros_like(ot)
            qt[...] = jnp.zeros_like(qt)
            whole(lambda body, carry: lax.fori_loop(0, steps, body, carry))

        lax.switch(
            jnp.minimum(steps - 1, UNROLLED), [unrolled(c + 1) for c in range(UNROLLED)] + [looped]
        )
        return 0

    lax.fori_loop(0, TILES // PAIR, q_tiles, 0)
    left_kv_ref[0] = (dk[0:MOST, :] * SCALE).astype(jnp.bfloat16)
    left_kv_ref[1] = dv[0:MOST, :].astype(jnp.bfloat16)
    right_kv_ref[0] = (dk[MOST + GROUP_ROWS : EXT_ROWS, :] * SCALE).astype(jnp.bfloat16)
    right_kv_ref[1] = dv[MOST + GROUP_ROWS : EXT_ROWS, :].astype(jnp.bfloat16)
    own_kv_ref[0] = dk[MOST : MOST + GROUP_ROWS, :] * SCALE
    own_kv_ref[1] = dv[MOST : MOST + GROUP_ROWS, :]


def attend(lo, hi, start, end, own, left, right, qg):
    smem = pl.BlockSpec(memory_space=pltpu.SMEM)
    vmem = pl.BlockSpec(memory_space=pltpu.VMEM)
    bf16, f32 = jnp.bfloat16, jnp.float32
    return pl.pallas_call(
        attend_kernel,
        out_shape=(
            jax.ShapeDtypeStruct((GROUP, 2 * ROWS, LANES), bf16),
            jax.ShapeDtypeStruct((2, GROUP_ROWS, LANES), f32),
            jax.ShapeDtypeStruct((2, MOST, LANES), bf16),
            jax.ShapeDtypeStruct((2, MOST, LANES), bf16),
        ),
        in_specs=[smem, smem] + [vmem] * 6,
        out_specs=(vmem,) * 4,
        scratch_shapes=[
            pltpu.VMEM((PAD_ROWS, LANES), bf16),
            pltpu.VMEM((PAD_ROWS, LANES), bf16),
            pltpu.VMEM((LANES, PAD_ROWS), bf16),
            pltpu.VMEM((LANES, PAD_ROWS), bf16),
            pltpu.VMEM((PAD_ROWS, LANES), f32),
            pltpu.VMEM((PAD_ROWS, LANES), f32),
            pltpu.VMEM((PAIR, MAX_STEPS * K_STEP, 2 * LANES), f32),
            pltpu.VMEM((PAIR, MAX_STEPS * K_STEP, 2 * LANES), f32),
            pltpu.VMEM((PAIR, LANES, LANES), f32),
            pltpu.VMEM((PAIR, LANES, LANES), f32),
        ],
        compiler_params=pltpu.CompilerParams(vmem_limit_bytes=48 * 1024 * 1024),
        cost_estimate=pl.CostEstimate(
            flops=20_000_000_000, bytes_accessed=12_000_000, transcendentals=6_000_000
        ),
        name="attend",
    )(lo, hi, start, end, own, left, right, qg)


def pack_kernel(*refs):
    for j in range(GROUP):
        at = 0
        for ref in refs[:-1]:
            rows = ref.shape[0]
            cols = slice(j * LANES, (j + 1) * LANES) if ref.shape[1] == D else slice(None)
            refs[-1][j, at : at + rows, :] = ref[:, cols]
            at += rows


def pack(*sources):
    rows = sum(x.shape[0] for x in sources)
    return pl.pallas_call(
        pack_kernel,
        out_shape=jax.ShapeDtypeStruct((GROUP, rows, LANES), jnp.bfloat16),
        cost_estimate=pl.CostEstimate(flops=0, bytes_accessed=3_200_000, transcendentals=0),
        name="pack",
    )(*sources)


def unpack_kernel(in_ref, x_ref, y_ref):
    for j in range(GROUP):
        cols = slice(j * LANES, (j + 1) * LANES)
        x_ref[:, cols] = in_ref[j, 0:ROWS, :]
        y_ref[:, cols] = in_ref[j, ROWS : 2 * ROWS, :]


def unpack(x):
    flat = jax.ShapeDtypeStruct((ROWS, D), jnp.bfloat16)
    return pl.pallas_call(
        unpack_kernel,
        out_shape=(flat, flat),
        cost_estimate=pl.CostEstimate(flops=0, bytes_accessed=3_200_000, transcendentals=0),
        name="unpack",
    )(x)


def total_kernel(own_ref, prev_ref, next_ref, out_ref):
    for n in range(2):
        for j in range(GROUP):
            x = own_ref[n, j * ROWS : (j + 1) * ROWS, :]
            if j < REACH:
                x = x + prev_ref[n, j * ROWS : (j + 1) * ROWS, :].astype(jnp.float32)
            if j >= GROUP - REACH:
                at = (j - GROUP + REACH) * ROWS
                x = x + next_ref[n, at : at + ROWS, :].astype(jnp.float32)
            out_ref[j, n * ROWS : (n + 1) * ROWS, :] = x.astype(jnp.bfloat16)


def total(own, from_prev, from_next):
    return pl.pallas_call(
        total_kernel,
        out_shape=jax.ShapeDtypeStruct((GROUP, 2 * ROWS, LANES), jnp.bfloat16),
        cost_estimate=pl.CostEstimate(flops=0, bytes_accessed=6_000_000, transcendentals=0),
        name="total",
    )(own, from_prev, from_next)


def exchange(x):
    return lax.all_to_all(x, "img", 0, 0, axis_index_groups=group_lists())


def bounds(own, left, right):
    def tags_of(x):
        return x[:, 2 * ROWS : 2 * ROWS + ROWS // LANES, :].astype(jnp.int32).reshape(-1)

    own_tags = tags_of(own)
    is_last = lax.axis_index("img") >= N_IMG - GROUP
    right_tags = jnp.where(is_last, N_IMG + 1, tags_of(right))
    ext_tags = jnp.concatenate([tags_of(left), own_tags, right_tags])
    every = jnp.arange(N_IMG + 1, dtype=jnp.int32)
    below = jnp.sum((ext_tags[None, :] < every[:, None]).astype(jnp.int32), 1)
    upto = jnp.sum((ext_tags[None, :] <= every[:, None]).astype(jnp.int32), 1)
    pick = own_tags[:, None] == every[None, :]
    start = jnp.sum(jnp.where(pick, below[None, :], 0), 1).reshape(TILES, LANES)
    end = jnp.sum(jnp.where(pick, upto[None, :], 0), 1).reshape(TILES, LANES)
    return start[:, 0], end[:, LANES - 1], start, end


def shards(queries, keys, values, out_grad, image_ids):
    tags = (image_ids + 1).astype(jnp.bfloat16).reshape(ROWS // LANES, LANES)
    tags = jnp.pad(tags, ((0, TAG_ROWS - ROWS // LANES), (0, 0)))
    kv, qg = lax.optimization_barrier((pack(keys, values, tags), pack(queries, out_grad)))
    own = exchange(kv)
    qg = exchange(qg)
    left = shifted(own[GROUP - REACH :], GROUP)
    right = shifted(own[:REACH], -GROUP)
    table = bounds(own, left, right)
    oq, own_kv, left_kv, right_kv = attend(*table, own, left, right, qg)
    oq = exchange(oq)
    from_next = shifted(left_kv, -GROUP)
    from_prev = shifted(right_kv, GROUP)
    attended, query_grad = unpack(oq)
    kv = exchange(total(own_kv, from_prev, from_next))
    key_grad, value_grad = unpack(kv)
    return attended, query_grad, key_grad, value_grad


def solution(mesh):
    in_specs = (P("img", None), P("img", None), P("img", None), P("img", None), P("img"))
    out_specs = (P("img", None), P("img", None), P("img", None), P("img", None))
    return jax.shard_map(shards, mesh=mesh, in_specs=in_specs, out_specs=out_specs, check_vma=False)
```

time: 217 us -> 167 us (0.77)
  the two profiles are of different devices: /device:TPU:2 before, /device:TPU:38 now
where the time goes in v2:
time: 167 us; the launch traced here: 166 us
  waiting for transfers between devices  52.9 us (32%)
  Pallas kernels  50.6 us (30%)
  starting transfers between devices  29.3 us (18%)
  blocking collectives  26.6 us (16%)
  local copies, waits for them, and re-layouts  3.42 us (2%)
  other arithmetic  2.73 us (2%)
    pallas_call x1, Pallas kernels, attend(): pl.pallas_call(attend_kernel, out_shape=(jax.ShapeDtypeStruct((GROUP, 2 *...  35.4 us
    all_to_all x3, waiting for transfers between devices, exchange(): return lax.all_to_all(x, 'img', 0, 0, axis_index_groups=group_lists())  27.3 us
    all_to_all x1, blocking collectives, exchange(): return lax.all_to_all(x, 'img', 0, 0, axis_index_groups=group_lists())  26.6 us
    ppermute x4, waiting for transfers between devices, shifted(): lax.ppermute(value, 'img', [(s, s + steps) for s in range(leading, last)])  25.6 us
    ppermute x4, starting transfers between devices, shifted(): lax.ppermute(value, 'img', [(s, s + steps) for s in range(leading, last)])  17.5 us
    all_to_all x3, starting transfers between devices, exchange(): return lax.all_to_all(x, 'img', 0, 0, axis_index_groups=group_lists())  11.8 us
    pallas_call x2, Pallas kernels, unpack(): pl.pallas_call(unpack_kernel, out_shape=(flat, flat), cost_estimate=pl.Co...  5.99 us
    pallas_call x2, Pallas kernels, pack(): pl.pallas_call(pack_kernel, out_shape=jax.ShapeDtypeStruct((GROUP, rows,...  5.65 us
  transfers between devices with their start and end apart: 7, of which 6 were waited for; matrix products, arithmetic and copies ran while one was open for 1% of the time, Pallas kernels for 4%

profile of v2, /device:TPU:38, one launch (start us, length us, event | category | flops | bytes accessed | tf_op | source)
XLA Modules:
  0.0 166.2 jit_solution(7893064138676024695)
XLA Ops:
  1.9 2.8 %pack.3 = bf16[8,768,128]{2,1,0:T(8,128)(2,1)} custom-call(bf16[384,1024]{1,0:T(8,128)(2,1)} %refs_0_.3, bf16[384,1024]{1,0:T(8,128)(2,1)} %refs_1_.3), custom_call_target="tpu_custom_call" | custom-call | bytes 3200000 | tf_op jit(solution)/shard_map/pack/pallas_call | solution.py:255
  4.7 2.8 %pack.2 = bf16[8,784,128]{2,1,0:T(8,128)(2,1)} custom-call(bf16[384,1024]{1,0:T(8,128)(2,1)} %refs_0_.2, bf16[384,1024]{1,0:T(8,128)(2,1)} %refs_1_.2, bf16[16,128]{1,0:T(8,128)(2,1)} %pad.4.refs_2_), custom_call_target="tpu_custom_call" | custom-call | bytes 3200000 | tf_op jit(solution)/shard_map/pack/pallas_call | solution.py:255
  7.6 26.6 %all_to_all.20.own_ref = bf16[8,784,128]{2,1,0:T(8,128)(2,1)S(1)} all-to-all(bf16[8,784,128]{2,1,0:T(8,128)(2,1)} %pack.2), channel_id=1, replica_groups={{0,1,2,3,4,5,6,7},{8,9,10,11,12,13,14,15},{16,17,18,19,20,21,22,23},{24..., dimensions={0} | all-to-all | bytes 3211264 | tf_op jit(solution)/shard_map/all_to_all | solution.py:302
  34.2 1.0 fusion.1
  35.2 3.8 %collective-permute-start = (bf16[3,784,128]{2,1,0:T(8,128)(2,1)}, bf16[3,784,128]{2,1,0:T(8,128)(2,1)S(1)}, u32[]{:S(2)}, u32[]{:S(2)}) collective-permute-start(bf16[3,784,128]{2,1,0:T(8,128)(2,1)} %get-tuple-element.28), channel_id=1, source_target_pairs={{0,8},{1,9},{2,10},{3,11},{4,12},{5,13},{6,14},{7,15},{8,16},{9,17... | collective-permute-start | bytes 1806344 | tf_op jit(solution)/shard_map/ppermute | solution.py:39
  39.0 2.0 %collective-permute-start.1 = (bf16[3,784,128]{2,1,0:T(8,128)(2,1)S(1)}, bf16[3,784,128]{2,1,0:T(8,128)(2,1)S(1)}, u32[]{:S(2)}, u32[]{:S(2)}) collective-permute-start(bf16[3,784,128]{2,1,0:T(8,128)(2,1)S(1)} %get-tuple-element.29), channel_id=1, source_target_pairs={{8,0},{9,1},{10,2},{11,3},{12,4},{13,5},{14,6},{15,7},{16,8},{17,9... | collective-permute-start | bytes 1806344 | tf_op jit(solution)/shard_map/ppermute | solution.py:39
  41.0 3.6 %all-to-all-start.1 = ((bf16[8,768,128]{2,1,0:T(8,128)(2,1)}), bf16[8,768,128]{2,1,0:T(8,128)(2,1)S(1)}, u32[]{:S(2)}, u32[]{:S(2)}) async-start(bf16[8,768,128]{2,1,0:T(8,128)(2,1)} %pack.3), calls=%async_computation.1 | async-start | bytes 3145728 | tf_op jit(solution)/shard_map/all_to_all | solution.py:302
  45.4 7.3 %collective-permute-done.left_ref = bf16[3,784,128]{2,1,0:T(8,128)(2,1)S(1)} collective-permute-done((bf16[3,784,128]{2,1,0:T(8,128)(2,1)}, bf16[3,784,128]{2,1,0:T(8,128)(2,1)S(1)}, u32[]{:S(2)}, u32[]{:S(2)}) %collective-permute-start) | collective-permute-done | bytes 602144 | tf_op jit(solution)/shard_map/ppermute | solution.py:39
  52.7 3.3 %collective-permute-done.1.right_ref = bf16[3,784,128]{2,1,0:T(8,128)(2,1)S(1)} collective-permute-done((bf16[3,784,128]{2,1,0:T(8,128)(2,1)S(1)}, bf16[3,784,128]{2,1,0:T(8,128)(2,1)S(1)}, u32[]{:S(2)}, u32[]{:S(2)}) %collective-permute-start.1) | collective-permute-done | bytes 602144 | tf_op jit(solution)/shard_map/ppermute | solution.py:39
  56.1 0.8 convert_reduce_fusion
  57.5 8.6 %all-to-all-done.1.qg_ref = bf16[8,768,128]{2,1,0:T(8,128)(2,1)S(1)} async-done(((bf16[8,768,128]{2,1,0:T(8,128)(2,1)}), bf16[8,768,128]{2,1,0:T(8,128)(2,1)S(1)}, u32[]{:S(2)}, u32[]{:S(2)}) %all-to-all-start.1) | async-done | bytes 1572896 | tf_op jit(solution)/shard_map/all_to_all | solution.py:302
  66.1 35.4 %attend.1 = (bf16[8,768,128]{2,1,0:T(8,128)(2,1)}, f32[2,3072,128]{2,1,0:T(8,128)}, bf16[2,1152,128]{2,1,0:T(8,128)(2,1)S(1)}, bf16[2,1152,128]{2,1,0:T(8,128)(2,1)S(1)}) custom-call(s32[24]{0:T(128)S(1)} %get-tuple-element.31.lo_ref, s32[24]{0:T(128)S(1)} %get-tuple-element.30.hi_ref, s32[24,128]{1,0:T(8,128)S(1)} %bitcast.7, s32[24,128]{1,0:T(8,128)S(1)} %bitcast.5, ...), custom_call_target="tpu_custom_call" | custom-call | flops 20000000000 | bytes 12000000 | tf_op jit(solution)/shard_map/attend/pallas_call | solution.py:213
  101.5 0.8 copy-done
  102.3 3.7 %all-to-all-start.2 = ((bf16[8,768,128]{2,1,0:T(8,128)(2,1)}), bf16[8,768,128]{2,1,0:T(8,128)(2,1)S(1)}, u32[]{:S(2)}, u32[]{:S(2)}) async-start(bf16[8,768,128]{2,1,0:T(8,128)(2,1)} %get-tuple-element.16), calls=%async_computation.2 | async-start | bytes 3145728 | tf_op jit(solution)/shard_map/all_to_all | solution.py:302
  106.0 9.5 %collective-permute-start.2 = (bf16[2,1152,128]{2,1,0:T(8,128)(2,1)S(1)}, bf16[2,1152,128]{2,1,0:T(8,128)(2,1)S(1)}, u32[]{:S(2)}, u32[]{:S(2)}) collective-permute-start(bf16[2,1152,128]{2,1,0:T(8,128)(2,1)S(1)} %copy-done.1), channel_id=1, source_target_pairs={{0,8},{1,9},{2,10},{3,11},{4,12},{5,13},{6,14},{7,15},{8,16},{9,17... | collective-permute-start | bytes 1769480 | tf_op jit(solution)/shard_map/ppermute | solution.py:39
  115.5 2.3 %collective-permute-start.3 = (bf16[2,1152,128]{2,1,0:T(8,128)(2,1)S(1)}, bf16[2,1152,128]{2,1,0:T(8,128)(2,1)S(1)}, u32[]{:S(2)}, u32[]{:S(2)}) collective-permute-start(bf16[2,1152,128]{2,1,0:T(8,128)(2,1)S(1)} %get-tuple-element.21), channel_id=1, source_target_pairs={{8,0},{9,1},{10,2},{11,3},{12,4},{13,5},{14,6},{15,7},{16,8},{17,9... | collective-permute-start | bytes 1769480 | tf_op jit(solution)/shard_map/ppermute | solution.py:39
  117.7 11.9 %collective-permute-done.2.prev_ref = bf16[2,1152,128]{2,1,0:T(8,128)(2,1)S(1)} collective-permute-done((bf16[2,1152,128]{2,1,0:T(8,128)(2,1)S(1)}, bf16[2,1152,128]{2,1,0:T(8,128)(2,1)S(1)}, u32[]{:S(2)}, u32[]{:S(2)}) %collective-permute-start.2) | collective-permute-done | bytes 589856 | tf_op jit(solution)/shard_map/ppermute | solution.py:39
  129.7 3.0 %collective-permute-done.3.next_ref = bf16[2,1152,128]{2,1,0:T(8,128)(2,1)S(1)} collective-permute-done((bf16[2,1152,128]{2,1,0:T(8,128)(2,1)S(1)}, bf16[2,1152,128]{2,1,0:T(8,128)(2,1)S(1)}, u32[]{:S(2)}, u32[]{:S(2)}) %collective-permute-start.3) | collective-permute-done | bytes 589856 | tf_op jit(solution)/shard_map/ppermute | solution.py:39
  132.7 0.8 copy-done.5
  133.5 3.6 %total.1 = bf16[8,768,128]{2,1,0:T(8,128)(2,1)} custom-call(f32[2,3072,128]{2,1,0:T(8,128)} %get-tuple-element.19.own_ref, bf16[2,1152,128]{2,1,0:T(8,128)(2,1)} %copy-done.4, bf16[2,1152,128]{2,1,0:T(8,128)(2,1)} %copy-done.5), custom_call_target="tpu_custom_call" | custom-call | bytes 6000000 | tf_op jit(solution)/shard_map/total/pallas_call | solution.py:293
  137.1 4.5 %all-to-all-start.3 = ((bf16[8,768,128]{2,1,0:T(8,128)(2,1)}), bf16[8,768,128]{2,1,0:T(8,128)(2,1)}, u32[]{:S(2)}, u32[]{:S(2)}) async-start(bf16[8,768,128]{2,1,0:T(8,128)(2,1)} %total.1), calls=%async_computation.3 | async-start | bytes 3145728 | tf_op jit(solution)/shard_map/all_to_all | solution.py:302
  141.6 3.0 %unpack.2 = (bf16[384,1024]{1,0:T(8,128)(2,1)}, bf16[384,1024]{1,0:T(8,128)(2,1)}) custom-call(bf16[8,768,128]{2,1,0:T(8,128)(2,1)} %copy-done.2), custom_call_target="tpu_custom_call" | custom-call | bytes 3200000 | tf_op jit(solution)/shard_map/unpack/pallas_call | solution.py:272
  144.6 18.7 %all-to-all-done.3.in_ref = bf16[8,768,128]{2,1,0:T(8,128)(2,1)} async-done(((bf16[8,768,128]{2,1,0:T(8,128)(2,1)}), bf16[8,768,128]{2,1,0:T(8,128)(2,1)}, u32[]{:S(2)}, u32[]{:S(2)}) %all-to-all-start.3) | async-done | bytes 1572896 | tf_op jit(solution)/shard_map/all_to_all | solution.py:302
  163.2 3.0 %unpack.3 = (bf16[384,1024]{1,0:T(8,128)(2,1)}, bf16[384,1024]{1,0:T(8,128)(2,1)}) custom-call(bf16[8,768,128]{2,1,0:T(8,128)(2,1)} %all-to-all-done.3.in_ref), custom_call_target="tpu_custom_call" | custom-call | bytes 3200000 | tf_op jit(solution)/shard_map/unpack/pallas_call | solution.py:272
  (22 shorter events, 2.7 us)
Async XLA Ops:
  34.2 4.8 %copy-start.3 = (bf16[8,784,128]{2,1,0:T(8,128)(2,1)}, bf16[8,784,128]{2,1,0:T(8,128)(2,1)S(1)}, u32[]{:S(2)}) copy-start(bf16[8,784,128]{2,1,0:T(8,128)(2,1)S(1)} %all_to_all.20.own_ref) | copy-start | bytes 4816900
  35.2 17.5 %collective-permute-start = (bf16[3,784,128]{2,1,0:T(8,128)(2,1)}, bf16[3,784,128]{2,1,0:T(8,128)(2,1)S(1)}, u32[]{:S(2)}, u32[]{:S(2)}) collective-permute-start(bf16[3,784,128]{2,1,0:T(8,128)(2,1)} %get-tuple-element.28), channel_id=1, source_target_pairs={{0,8},{1,9},{2,10},{3,11},{4,12},{5,13},{6,14},{7,15},{8,16},{9,17... | collective-permute-start | bytes 1806344 | tf_op jit(solution)/shard_map/ppermute | solution.py:39
  39.0 17.0 %collective-permute-start.1 = (bf16[3,784,128]{2,1,0:T(8,128)(2,1)S(1)}, bf16[3,784,128]{2,1,0:T(8,128)(2,1)S(1)}, u32[]{:S(2)}, u32[]{:S(2)}) collective-permute-start(bf16[3,784,128]{2,1,0:T(8,128)(2,1)S(1)} %get-tuple-element.29), channel_id=1, source_target_pairs={{8,0},{9,1},{10,2},{11,3},{12,4},{13,5},{14,6},{15,7},{16,8},{17,9... | collective-permute-start | bytes 1806344 | tf_op jit(solution)/shard_map/ppermute | solution.py:39
  41.0 25.1 %all-to-all-start.1 = ((bf16[8,768,128]{2,1,0:T(8,128)(2,1)}), bf16[8,768,128]{2,1,0:T(8,128)(2,1)S(1)}, u32[]{:S(2)}, u32[]{:S(2)}) async-start(bf16[8,768,128]{2,1,0:T(8,128)(2,1)} %pack.3), calls=%async_computation.1 | async-start | bytes 3145728 | tf_op jit(solution)/shard_map/all_to_all | solution.py:302
  101.5 0.8 copy-start
  102.3 3.7 %copy-start.1 = (bf16[2,1152,128]{2,1,0:T(8,128)(2,1)S(1)}, bf16[2,1152,128]{2,1,0:T(8,128)(2,1)}, u32[]{:S(2)}) copy-start(bf16[2,1152,128]{2,1,0:T(8,128)(2,1)} %copy-done) | copy-start | bytes 1769476
  102.3 34.8 %all-to-all-start.2 = ((bf16[8,768,128]{2,1,0:T(8,128)(2,1)}), bf16[8,768,128]{2,1,0:T(8,128)(2,1)S(1)}, u32[]{:S(2)}, u32[]{:S(2)}) async-start(bf16[8,768,128]{2,1,0:T(8,128)(2,1)} %get-tuple-element.16), calls=%async_computation.2 | async-start | bytes 3145728 | tf_op jit(solution)/shard_map/all_to_all | solution.py:302
  106.0 23.6 %collective-permute-start.2 = (bf16[2,1152,128]{2,1,0:T(8,128)(2,1)S(1)}, bf16[2,1152,128]{2,1,0:T(8,128)(2,1)S(1)}, u32[]{:S(2)}, u32[]{:S(2)}) collective-permute-start(bf16[2,1152,128]{2,1,0:T(8,128)(2,1)S(1)} %copy-done.1), channel_id=1, source_target_pairs={{0,8},{1,9},{2,10},{3,11},{4,12},{5,13},{6,14},{7,15},{8,16},{9,17... | collective-permute-start | bytes 1769480 | tf_op jit(solution)/shard_map/ppermute | solution.py:39
  115.5 17.2 %collective-permute-start.3 = (bf16[2,1152,128]{2,1,0:T(8,128)(2,1)S(1)}, bf16[2,1152,128]{2,1,0:T(8,128)(2,1)S(1)}, u32[]{:S(2)}, u32[]{:S(2)}) collective-permute-start(bf16[2,1152,128]{2,1,0:T(8,128)(2,1)S(1)} %get-tuple-element.21), channel_id=1, source_target_pairs={{8,0},{9,1},{10,2},{11,3},{12,4},{13,5},{14,6},{15,7},{16,8},{17,9... | collective-permute-start | bytes 1769480 | tf_op jit(solution)/shard_map/ppermute | solution.py:39
  129.7 3.9 %copy-start.4 = (bf16[2,1152,128]{2,1,0:T(8,128)(2,1)}, bf16[2,1152,128]{2,1,0:T(8,128)(2,1)S(1)}, u32[]{:S(2)}) copy-start(bf16[2,1152,128]{2,1,0:T(8,128)(2,1)S(1)} %collective-permute-done.2.prev_ref) | copy-start | bytes 1769476
  132.7 0.8 copy-start.5
  137.1 4.5 %copy-start.2 = (bf16[8,768,128]{2,1,0:T(8,128)(2,1)}, bf16[8,768,128]{2,1,0:T(8,128)(2,1)S(1)}, u32[]{:S(2)}) copy-start(bf16[8,768,128]{2,1,0:T(8,128)(2,1)S(1)} %all-to-all-done.2.in_ref) | copy-start | bytes 4718596
  137.1 26.2 %all-to-all-start.3 = ((bf16[8,768,128]{2,1,0:T(8,128)(2,1)}), bf16[8,768,128]{2,1,0:T(8,128)(2,1)}, u32[]{:S(2)}, u32[]{:S(2)}) async-start(bf16[8,768,128]{2,1,0:T(8,128)(2,1)} %total.1), calls=%async_computation.3 | async-start | bytes 3145728 | tf_op jit(solution)/shard_map/all_to_all | solution.py:302

commit v3 on v2

--- a/solution.py
+++ b/solution.py
@@ -22,6 +22,7 @@
 PAD_ROWS = EXT_ROWS + K_STEP
 TILES = GROUP_ROWS // LANES
 TAG_ROWS = 16
+Q_AT = 2 * ROWS + TAG_ROWS
 MAX_STEPS = 11
 UNROLLED = 8
 PAIR = 2
@@ -52,7 +53,7 @@
 
 
 def attend_kernel(
-    lo_ref, hi_ref, start_ref, end_ref, own_ref, left_ref, right_ref, qg_ref,
+    lo_ref, hi_ref, start_ref, end_ref, own_ref, left_ref, right_ref, g_ref,
     oq_ref, own_kv_ref, left_kv_ref, right_kv_ref,
     kx, vx, kt, vt, dk, dv, sbuf, dbuf, ot, qt,
 ):
@@ -78,7 +79,11 @@
         vt[:, pl.ds(at, K_STEP)] = vx[pl.ds(at, K_STEP), :].T
         return 0
 
-    lax.fori_loop(0, PAD_ROWS // K_STEP, transpose_chunk, 0)
+    first_chunk = lo_ref[0] // K_STEP
+    last_chunk = jnp.minimum(hi_ref[TILES - 1] // K_STEP + 2, PAD_ROWS // K_STEP)
+    kt[...] = jnp.zeros_like(kt)
+    vt[...] = jnp.zeros_like(vt)
+    lax.fori_loop(first_chunk, last_chunk, transpose_chunk, 0)
 
     lane = lax.broadcasted_iota(jnp.int32, (LANES, LANES), 1)
     first_head = lane < HEAD_DIM
@@ -105,8 +110,8 @@
 
         def tile_part(sub, run):
             j, t, dev, off, k0 = sub
-            q2 = both_heads(qg_ref[dev, pl.ds(off, LANES), :])
-            g2 = both_heads(qg_ref[dev, pl.ds(off + ROWS, LANES), :])
+            q2 = both_heads(own_ref[dev, pl.ds(pl.multiple_of(off + Q_AT, TAG_ROWS), LANES), :])
+            g2 = both_heads(g_ref[dev, pl.ds(off, LANES), :])
             begin = start_ref[pl.ds(t, 1), :]
             stop = end_ref[pl.ds(t, 1), :]
 
@@ -202,11 +207,11 @@
     left_kv_ref[1] = dv[0:MOST, :].astype(jnp.bfloat16)
     right_kv_ref[0] = (dk[MOST + GROUP_ROWS : EXT_ROWS, :] * SCALE).astype(jnp.bfloat16)
     right_kv_ref[1] = dv[MOST + GROUP_ROWS : EXT_ROWS, :].astype(jnp.bfloat16)
-    own_kv_ref[0] = dk[MOST : MOST + GROUP_ROWS, :] * SCALE
-    own_kv_ref[1] = dv[MOST : MOST + GROUP_ROWS, :]
-
-
-def attend(lo, hi, start, end, own, left, right, qg):
+    own_kv_ref[0] = (dk[MOST : MOST + GROUP_ROWS, :] * SCALE).astype(jnp.bfloat16)
+    own_kv_ref[1] = dv[MOST : MOST + GROUP_ROWS, :].astype(jnp.bfloat16)
+
+
+def attend(lo, hi, start, end, own, left, right, grad):
     smem = pl.BlockSpec(memory_space=pltpu.SMEM)
     vmem = pl.BlockSpec(memory_space=pltpu.VMEM)
     bf16, f32 = jnp.bfloat16, jnp.float32
@@ -214,7 +219,7 @@
         attend_kernel,
         out_shape=(
             jax.ShapeDtypeStruct((GROUP, 2 * ROWS, LANES), bf16),
-            jax.ShapeDtypeStruct((2, GROUP_ROWS, LANES), f32),
+            jax.ShapeDtypeStruct((2, GROUP_ROWS, LANES), bf16),
             jax.ShapeDtypeStruct((2, MOST, LANES), bf16),
             jax.ShapeDtypeStruct((2, MOST, LANES), bf16),
         ),
@@ -237,25 +242,31 @@
             flops=20_000_000_000, bytes_accessed=12_000_000, transcendentals=6_000_000
         ),
         name="attend",
-    )(lo, hi, start, end, own, left, right, qg)
-
-
-def pack_kernel(*refs):
+    )(lo, hi, start, end, own, left, right, grad)
+
+
+def pack_first_kernel(k_ref, v_ref, q_ref, id_ref, out_ref):
+    tags = (id_ref[...] + 1).astype(jnp.float32)
+    tags = jnp.concatenate([tags, jnp.zeros((TAG_ROWS - tags.shape[0], LANES), jnp.float32)], 0)
+    tags = tags.astype(jnp.bfloat16)
     for j in range(GROUP):
-        at = 0
-        for ref in refs[:-1]:
-            rows = ref.shape[0]
-            cols = slice(j * LANES, (j + 1) * LANES) if ref.shape[1] == D else slice(None)
-            refs[-1][j, at : at + rows, :] = ref[:, cols]
-            at += rows
-
-
-def pack(*sources):
-    rows = sum(x.shape[0] for x in sources)
+        cols = slice(j * LANES, (j + 1) * LANES)
+        out_ref[j, 0:ROWS, :] = k_ref[:, cols]
+        out_ref[j, ROWS : 2 * ROWS, :] = v_ref[:, cols]
+        out_ref[j, 2 * ROWS : Q_AT, :] = tags
+        out_ref[j, Q_AT : Q_AT + ROWS, :] = q_ref[:, cols]
+
+
+def pack_grad_kernel(g_ref, out_ref):
+    for j in range(GROUP):
+        out_ref[j] = g_ref[:, j * LANES : (j + 1) * LANES]
+
+
+def pack(kernel, rows, *sources):
     return pl.pallas_call(
-        pack_kernel,
+        kernel,
         out_shape=jax.ShapeDtypeStruct((GROUP, rows, LANES), jnp.bfloat16),
-        cost_estimate=pl.CostEstimate(flops=0, bytes_accessed=3_200_000, transcendentals=0),
+        cost_estimate=pl.CostEstimate(flops=0, bytes_accessed=rows * 4096, transcendentals=0),
         name="pack",
     )(*sources)
 
@@ -280,7 +291,7 @@
 def total_kernel(own_ref, prev_ref, next_ref, out_ref):
     for n in range(2):
         for j in range(GROUP):
-            x = own_ref[n, j * ROWS : (j + 1) * ROWS, :]
+            x = own_ref[n, j * ROWS : (j + 1) * ROWS, :].astype(jnp.float32)
             if j < REACH:
                 x = x + prev_ref[n, j * ROWS : (j + 1) * ROWS, :].astype(jnp.float32)
             if j >= GROUP - REACH:
@@ -320,15 +331,14 @@
 
 
 def shards(queries, keys, values, out_grad, image_ids):
-    tags = (image_ids + 1).astype(jnp.bfloat16).reshape(ROWS // LANES, LANES)
-    tags = jnp.pad(tags, ((0, TAG_ROWS - ROWS // LANES), (0, 0)))
-    kv, qg = lax.optimization_barrier((pack(keys, values, tags), pack(queries, out_grad)))
-    own = exchange(kv)
-    qg = exchange(qg)
-    left = shifted(own[GROUP - REACH :], GROUP)
-    right = shifted(own[:REACH], -GROUP)
+    ids = image_ids.reshape(ROWS // LANES, LANES)
+    own = exchange(pack(pack_first_kernel, Q_AT + ROWS, keys, values, queries, ids))
+    own, grad = lax.optimization_barrier((own, pack(pack_grad_kernel, ROWS, out_grad)))
+    left = shifted(own[GROUP - REACH :, :Q_AT], GROUP)
+    right = shifted(own[:REACH, :Q_AT], -GROUP)
+    grad = exchange(grad)
     table = bounds(own, left, right)
-    oq, own_kv, left_kv, right_kv = attend(*table, own, left, right, qg)
+    oq, own_kv, left_kv, right_kv = attend(*table, own, left, right, grad)
     oq = exchange(oq)
     from_next = shifted(left_kv, -GROUP)
     from_prev = shifted(right_kv, GROUP)

time: 167 us -> 167 us (level)
  waiting for transfers between devices: 52.9 us -> 82 us
  blocking collectives: 26.6 us -> 0 us
  Pallas kernels: 50.6 us -> 48.7 us
    all_to_all x1 -> x0, blocking collectives: 26.6 us -> none  [exchange(): return lax.all_to_all(x, 'img', 0, 0, axis_index_groups=group_lists())]
    all_to_all x3 -> x4, waiting for transfers between devices: 27.3 us -> 47.2 us  [exchange(): return lax.all_to_all(x, 'img', 0, 0, axis_index_groups=group_lists())]
    ppermute x4, waiting for transfers between devices: 25.6 us -> 34.8 us  [shifted(): lax.ppermute(value, 'img', [(s, s + steps) for s in range(leading, last)])]
    ppermute x4, starting transfers between devices: 17.5 us -> 11.8 us  [shifted(): lax.ppermute(value, 'img', [(s, s + steps) for s in range(leading, last)])]
    all_to_all x3 -> x4, starting transfers between devices: 11.8 us -> 16.1 us  [exchange(): return lax.all_to_all(x, 'img', 0, 0, axis_index_groups=group_lists())]
  transfers between devices with their start and end apart: 7 -> 8, of which waited for: 6 -> 7; matrix products, arithmetic and copies ran while one was open for 1% -> 1% of each run, Pallas kernels for 4% -> 5%
where the time goes in v3:
time: 167 us; the launch traced here: 165 us
  waiting for transfers between devices  82 us (49%)
  Pallas kernels  48.7 us (29%)
  starting transfers between devices  27.9 us (17%)
  local copies, waits for them, and re-layouts  3.78 us (2%)
  other arithmetic  2.04 us (1%)
    all_to_all x4, waiting for transfers between devices, exchange(): return lax.all_to_all(x, 'img', 0, 0, axis_index_groups=group_lists())  47.2 us
    ppermute x4, waiting for transfers between devices, shifted(): lax.ppermute(value, 'img', [(s, s + steps) for s in range(leading, last)])  34.8 us
    pallas_call x1, Pallas kernels, attend(): pl.pallas_call(attend_kernel, out_shape=(jax.ShapeDtypeStruct((GROUP, 2 *...  33.9 us
    all_to_all x4, starting transfers between devices, exchange(): return lax.all_to_all(x, 'img', 0, 0, axis_index_groups=group_lists())  16.1 us
    ppermute x4, starting transfers between devices, shifted(): lax.ppermute(value, 'img', [(s, s + steps) for s in range(leading, last)])  11.8 us
    pallas_call x2, Pallas kernels, unpack(): pl.pallas_call(unpack_kernel, out_shape=(flat, flat), cost_estimate=pl.Co...  5.99 us
    pallas_call x2, Pallas kernels, pack(): pl.pallas_call(kernel, out_shape=jax.ShapeDtypeStruct((GROUP, rows, LANES...  5.68 us
  transfers between devices with their start and end apart: 8, of which 7 were waited for; matrix products, arithmetic and copies ran while one was open for 1% of the time, Pallas kernels for 5%

profile of v3, /device:TPU:38, one launch (start us, length us, event | category | flops | bytes accessed | tf_op | source)
XLA Modules:
  0.0 165.1 jit_solution(15286212525146328440)
XLA Ops:
  0.6 3.5 %pack.2 = bf16[8,1168,128]{2,1,0:T(8,128)(2,1)} custom-call(bf16[384,1024]{1,0:T(8,128)(2,1)} %k_ref.1, bf16[384,1024]{1,0:T(8,128)(2,1)} %v_ref.1, bf16[384,1024]{1,0:T(8,128)(2,1)} %q_ref.1, s32[3,128]{1,0:T(4,128)} %bitcast.7), custom_call_target="tpu_custom_call" | custom-call | bytes 4784128 | tf_op jit(solution)/shard_map/pack/pallas_call | solution.py:266
  4.2 4.5 %all-to-all-start = ((bf16[8,1168,128]{2,1,0:T(8,128)(2,1)}), bf16[8,1168,128]{2,1,0:T(8,128)(2,1)S(1)}, u32[]{:S(2)}, u32[]{:S(2)}) async-start(bf16[8,1168,128]{2,1,0:T(8,128)(2,1)} %pack.2), calls=%async_computation | async-start | bytes 4784128 | tf_op jit(solution)/shard_map/all_to_all | solution.py:313
  8.6 2.2 %pack.3 = bf16[8,384,128]{2,1,0:T(8,128)(2,1)} custom-call(bf16[384,1024]{1,0:T(8,128)(2,1)} %g_ref.1), custom_call_target="tpu_custom_call" | custom-call | bytes 1572864 | tf_op jit(solution)/shard_map/pack/pallas_call | solution.py:266
  10.8 28.2 %all-to-all-done.own_ref = bf16[8,1168,128]{2,1,0:T(8,128)(2,1)S(1)} async-done(((bf16[8,1168,128]{2,1,0:T(8,128)(2,1)}), bf16[8,1168,128]{2,1,0:T(8,128)(2,1)S(1)}, u32[]{:S(2)}, u32[]{:S(2)}) %all-to-all-start) | async-done | bytes 2392096 | tf_op jit(solution)/shard_map/all_to_all | solution.py:313
  39.0 1.0 fusion
  40.6 3.8 %collective-permute-start = (bf16[3,784,128]{2,1,0:T(8,128)(2,1)}, bf16[3,784,128]{2,1,0:T(8,128)(2,1)S(1)}, u32[]{:S(2)}, u32[]{:S(2)}) collective-permute-start(bf16[3,784,128]{2,1,0:T(8,128)(2,1)} %get-tuple-element.28), channel_id=1, source_target_pairs={{0,8},{1,9},{2,10},{3,11},{4,12},{5,13},{6,14},{7,15},{8,16},{9,17... | collective-permute-start | bytes 1806344 | tf_op jit(solution)/shard_map/ppermute | solution.py:40
  44.4 2.0 %collective-permute-start.1 = (bf16[3,784,128]{2,1,0:T(8,128)(2,1)S(1)}, bf16[3,784,128]{2,1,0:T(8,128)(2,1)S(1)}, u32[]{:S(2)}, u32[]{:S(2)}) collective-permute-start(bf16[3,784,128]{2,1,0:T(8,128)(2,1)S(1)} %get-tuple-element.29), channel_id=1, source_target_pairs={{8,0},{9,1},{10,2},{11,3},{12,4},{13,5},{14,6},{15,7},{16,8},{17,9... | collective-permute-start | bytes 1806344 | tf_op jit(solution)/shard_map/ppermute | solution.py:40
  46.5 3.6 %all-to-all-start.1 = ((bf16[8,384,128]{2,1,0:T(8,128)(2,1)}), bf16[8,384,128]{2,1,0:T(8,128)(2,1)S(1)}, u32[]{:S(2)}, u32[]{:S(2)}) async-start(bf16[8,384,128]{2,1,0:T(8,128)(2,1)} %pack.3), calls=%async_computation.1 | async-start | bytes 1572864 | tf_op jit(solution)/shard_map/all_to_all | solution.py:313
  50.8 7.1 %collective-permute-done.left_ref = bf16[3,784,128]{2,1,0:T(8,128)(2,1)S(1)} collective-permute-done((bf16[3,784,128]{2,1,0:T(8,128)(2,1)}, bf16[3,784,128]{2,1,0:T(8,128)(2,1)S(1)}, u32[]{:S(2)}, u32[]{:S(2)}) %collective-permute-start) | collective-permute-done | bytes 602144 | tf_op jit(solution)/shard_map/ppermute | solution.py:40
  57.8 3.3 %collective-permute-done.1.right_ref = bf16[3,784,128]{2,1,0:T(8,128)(2,1)S(1)} collective-permute-done((bf16[3,784,128]{2,1,0:T(8,128)(2,1)S(1)}, bf16[3,784,128]{2,1,0:T(8,128)(2,1)S(1)}, u32[]{:S(2)}, u32[]{:S(2)}) %collective-permute-start.1) | collective-permute-done | bytes 602144 | tf_op jit(solution)/shard_map/ppermute | solution.py:40
  61.2 0.9 convert_reduce_fusion
  63.1 33.9 %attend.1 = (bf16[8,768,128]{2,1,0:T(8,128)(2,1)}, bf16[2,3072,128]{2,1,0:T(8,128)(2,1)}, bf16[2,1152,128]{2,1,0:T(8,128)(2,1)S(1)}, bf16[2,1152,128]{2,1,0:T(8,128)(2,1)S(1)}) custom-call(s32[24]{0:T(128)S(1)} %get-tuple-element.31.lo_ref, s32[24]{0:T(128)S(1)} %get-tuple-element.30.hi_ref, s32[24,128]{1,0:T(8,128)S(1)} %bitcast.6, s32[24,128]{1,0:T(8,128)S(1)} %bitcast.4, ...), custom_call_target="tpu_custom_call" | custom-call | flops 20000000000 | bytes 12000000 | tf_op jit(solution)/shard_map/attend/pallas_call | solution.py:218
  97.0 3.6 %all-to-all-start.2 = ((bf16[8,768,128]{2,1,0:T(8,128)(2,1)}), bf16[8,768,128]{2,1,0:T(8,128)(2,1)S(1)}, u32[]{:S(2)}, u32[]{:S(2)}) async-start(bf16[8,768,128]{2,1,0:T(8,128)(2,1)} %get-tuple-element.16), calls=%async_computation.2 | async-start | bytes 3145728 | tf_op jit(solution)/shard_map/all_to_all | solution.py:313
  100.5 4.1 %collective-permute-start.2 = (bf16[2,1152,128]{2,1,0:T(8,128)(2,1)S(1)}, bf16[2,1152,128]{2,1,0:T(8,128)(2,1)S(1)}, u32[]{:S(2)}, u32[]{:S(2)}) collective-permute-start(bf16[2,1152,128]{2,1,0:T(8,128)(2,1)S(1)} %get-tuple-element.20), channel_id=1, source_target_pairs={{0,8},{1,9},{2,10},{3,11},{4,12},{5,13},{6,14},{7,15},{8,16},{9,17... | collective-permute-start | bytes 1769480 | tf_op jit(solution)/shard_map/ppermute | solution.py:40
  104.6 1.9 %collective-permute-start.3 = (bf16[2,1152,128]{2,1,0:T(8,128)(2,1)S(1)}, bf16[2,1152,128]{2,1,0:T(8,128)(2,1)S(1)}, u32[]{:S(2)}, u32[]{:S(2)}) collective-permute-start(bf16[2,1152,128]{2,1,0:T(8,128)(2,1)S(1)} %get-tuple-element.21), channel_id=1, source_target_pairs={{8,0},{9,1},{10,2},{11,3},{12,4},{13,5},{14,6},{15,7},{16,8},{17,9... | collective-permute-start | bytes 1769480 | tf_op jit(solution)/shard_map/ppermute | solution.py:40
  106.5 11.5 %collective-permute-done.2.prev_ref = bf16[2,1152,128]{2,1,0:T(8,128)(2,1)S(1)} collective-permute-done((bf16[2,1152,128]{2,1,0:T(8,128)(2,1)S(1)}, bf16[2,1152,128]{2,1,0:T(8,128)(2,1)S(1)}, u32[]{:S(2)}, u32[]{:S(2)}) %collective-permute-start.2) | collective-permute-done | bytes 589856 | tf_op jit(solution)/shard_map/ppermute | solution.py:40
  118.1 12.9 %collective-permute-done.3.next_ref = bf16[2,1152,128]{2,1,0:T(8,128)(2,1)S(1)} collective-permute-done((bf16[2,1152,128]{2,1,0:T(8,128)(2,1)S(1)}, bf16[2,1152,128]{2,1,0:T(8,128)(2,1)S(1)}, u32[]{:S(2)}, u32[]{:S(2)}) %collective-permute-start.3) | collective-permute-done | bytes 589856 | tf_op jit(solution)/shard_map/ppermute | solution.py:40
  131.0 0.8 copy-done.4
  131.8 3.2 %total.1 = bf16[8,768,128]{2,1,0:T(8,128)(2,1)} custom-call(bf16[2,3072,128]{2,1,0:T(8,128)(2,1)} %get-tuple-element.19.own_ref, bf16[2,1152,128]{2,1,0:T(8,128)(2,1)} %copy-done.3, bf16[2,1152,128]{2,1,0:T(8,128)(2,1)} %copy-done.4), custom_call_target="tpu_custom_call" | custom-call | bytes 6000000 | tf_op jit(solution)/shard_map/total/pallas_call | solution.py:304
  134.9 4.5 %all-to-all-start.3 = ((bf16[8,768,128]{2,1,0:T(8,128)(2,1)}), bf16[8,768,128]{2,1,0:T(8,128)(2,1)S(1)}, u32[]{:S(2)}, u32[]{:S(2)}) async-start(bf16[8,768,128]{2,1,0:T(8,128)(2,1)} %total.1), calls=%async_computation.3 | async-start | bytes 3145728 | tf_op jit(solution)/shard_map/all_to_all | solution.py:313
  139.4 3.0 %unpack.2 = (bf16[384,1024]{1,0:T(8,128)(2,1)}, bf16[384,1024]{1,0:T(8,128)(2,1)}) custom-call(bf16[8,768,128]{2,1,0:T(8,128)(2,1)} %copy-done), custom_call_target="tpu_custom_call" | custom-call | bytes 3200000 | tf_op jit(solution)/shard_map/unpack/pallas_call | solution.py:283
  142.4 18.6 %all-to-all-done.3.in_ref = bf16[8,768,128]{2,1,0:T(8,128)(2,1)S(1)} async-done(((bf16[8,768,128]{2,1,0:T(8,128)(2,1)}), bf16[8,768,128]{2,1,0:T(8,128)(2,1)S(1)}, u32[]{:S(2)}, u32[]{:S(2)}) %all-to-all-start.3) | async-done | bytes 1572896 | tf_op jit(solution)/shard_map/all_to_all | solution.py:313
  161.0 1.2 copy-done.1
  162.1 3.0 %unpack.3 = (bf16[384,1024]{1,0:T(8,128)(2,1)}, bf16[384,1024]{1,0:T(8,128)(2,1)}) custom-call(bf16[8,768,128]{2,1,0:T(8,128)(2,1)} %copy-done.1), custom_call_target="tpu_custom_call" | custom-call | bytes 3200000 | tf_op jit(solution)/shard_map/unpack/pallas_call | solution.py:283
  (19 shorter events, 2.4 us)
Async XLA Ops:
  4.2 34.8 %all-to-all-start = ((bf16[8,1168,128]{2,1,0:T(8,128)(2,1)}), bf16[8,1168,128]{2,1,0:T(8,128)(2,1)S(1)}, u32[]{:S(2)}, u32[]{:S(2)}) async-start(bf16[8,1168,128]{2,1,0:T(8,128)(2,1)} %pack.2), calls=%async_computation | async-start | bytes 4784128 | tf_op jit(solution)/shard_map/all_to_all | solution.py:313
  39.0 1.6 copy-start.2
  40.6 17.2 %collective-permute-start = (bf16[3,784,128]{2,1,0:T(8,128)(2,1)}, bf16[3,784,128]{2,1,0:T(8,128)(2,1)S(1)}, u32[]{:S(2)}, u32[]{:S(2)}) collective-permute-start(bf16[3,784,128]{2,1,0:T(8,128)(2,1)} %get-tuple-element.28), channel_id=1, source_target_pairs={{0,8},{1,9},{2,10},{3,11},{4,12},{5,13},{6,14},{7,15},{8,16},{9,17... | collective-permute-start | bytes 1806344 | tf_op jit(solution)/shard_map/ppermute | solution.py:40
  44.4 16.7 %collective-permute-start.1 = (bf16[3,784,128]{2,1,0:T(8,128)(2,1)S(1)}, bf16[3,784,128]{2,1,0:T(8,128)(2,1)S(1)}, u32[]{:S(2)}, u32[]{:S(2)}) collective-permute-start(bf16[3,784,128]{2,1,0:T(8,128)(2,1)S(1)} %get-tuple-element.29), channel_id=1, source_target_pairs={{8,0},{9,1},{10,2},{11,3},{12,4},{13,5},{14,6},{15,7},{16,8},{17,9... | collective-permute-start | bytes 1806344 | tf_op jit(solution)/shard_map/ppermute | solution.py:40
  46.5 16.6 %all-to-all-start.1 = ((bf16[8,384,128]{2,1,0:T(8,128)(2,1)}), bf16[8,384,128]{2,1,0:T(8,128)(2,1)S(1)}, u32[]{:S(2)}, u32[]{:S(2)}) async-start(bf16[8,384,128]{2,1,0:T(8,128)(2,1)} %pack.3), calls=%async_computation.1 | async-start | bytes 1572864 | tf_op jit(solution)/shard_map/all_to_all | solution.py:313
  97.0 38.0 %all-to-all-start.2 = ((bf16[8,768,128]{2,1,0:T(8,128)(2,1)}), bf16[8,768,128]{2,1,0:T(8,128)(2,1)S(1)}, u32[]{:S(2)}, u32[]{:S(2)}) async-start(bf16[8,768,128]{2,1,0:T(8,128)(2,1)} %get-tuple-element.16), calls=%async_computation.2 | async-start | bytes 3145728 | tf_op jit(solution)/shard_map/all_to_all | solution.py:313
  100.5 17.5 %collective-permute-start.2 = (bf16[2,1152,128]{2,1,0:T(8,128)(2,1)S(1)}, bf16[2,1152,128]{2,1,0:T(8,128)(2,1)S(1)}, u32[]{:S(2)}, u32[]{:S(2)}) collective-permute-start(bf16[2,1152,128]{2,1,0:T(8,128)(2,1)S(1)} %get-tuple-element.20), channel_id=1, source_target_pairs={{0,8},{1,9},{2,10},{3,11},{4,12},{5,13},{6,14},{7,15},{8,16},{9,17... | collective-permute-start | bytes 1769480 | tf_op jit(solution)/shard_map/ppermute | solution.py:40
  104.6 26.3 %collective-permute-start.3 = (bf16[2,1152,128]{2,1,0:T(8,128)(2,1)S(1)}, bf16[2,1152,128]{2,1,0:T(8,128)(2,1)S(1)}, u32[]{:S(2)}, u32[]{:S(2)}) collective-permute-start(bf16[2,1152,128]{2,1,0:T(8,128)(2,1)S(1)} %get-tuple-element.21), channel_id=1, source_target_pairs={{8,0},{9,1},{10,2},{11,3},{12,4},{13,5},{14,6},{15,7},{16,8},{17,9... | collective-permute-start | bytes 1769480 | tf_op jit(solution)/shard_map/ppermute | solution.py:40
  118.1 12.9 %copy-start.3 = (bf16[2,1152,128]{2,1,0:T(8,128)(2,1)}, bf16[2,1152,128]{2,1,0:T(8,128)(2,1)S(1)}, u32[]{:S(2)}) copy-start(bf16[2,1152,128]{2,1,0:T(8,128)(2,1)S(1)} %collective-permute-done.2.prev_ref) | copy-start | bytes 1769476
  130.9 0.8 copy-start.4
  134.9 4.5 %copy-start = (bf16[8,768,128]{2,1,0:T(8,128)(2,1)}, bf16[8,768,128]{2,1,0:T(8,128)(2,1)S(1)}, u32[]{:S(2)}) copy-start(bf16[8,768,128]{2,1,0:T(8,128)(2,1)S(1)} %all-to-all-done.2.in_ref) | copy-start | bytes 4718596
  134.9 26.1 %all-to-all-start.3 = ((bf16[8,768,128]{2,1,0:T(8,128)(2,1)}), bf16[8,768,128]{2,1,0:T(8,128)(2,1)S(1)}, u32[]{:S(2)}, u32[]{:S(2)}) async-start(bf16[8,768,128]{2,1,0:T(8,128)(2,1)} %total.1), calls=%async_computation.3 | async-start | bytes 3145728 | tf_op jit(solution)/shard_map/all_to_all | solution.py:313
  161.0 1.2 copy-start.1

commit v4 on v3

--- a/solution.py
+++ b/solution.py
@@ -23,7 +23,7 @@
 TILES = GROUP_ROWS // LANES
 TAG_ROWS = 16
 Q_AT = 2 * ROWS + TAG_ROWS
-MAX_STEPS = 11
+MAX_STEPS = 12
 UNROLLED = 8
 PAIR = 2
 SCALE = 1.0 / math.sqrt(HEAD_DIM)
@@ -101,12 +101,12 @@
         steps = step_count(tiles[0])
         for t in tiles[1:]:
             steps = jnp.maximum(steps, step_count(t))
-        subs = []
-        for j, t in enumerate(tiles):
+
+        def sub_of(j, t, reach):
             dev = t // REACH
             off = pl.multiple_of((t % REACH) * LANES, LANES)
-            k0 = jnp.minimum((lo_ref[t] // LANES) * LANES, PAD_ROWS - steps * K_STEP)
-            subs.append((j, t, dev, off, k0))
+            k0 = jnp.minimum((lo_ref[t] // LANES) * LANES, PAD_ROWS - reach * K_STEP)
+            return j, t, dev, off, k0
 
         def tile_part(sub, run):
             j, t, dev, off, k0 = sub
@@ -178,7 +178,7 @@
             return first, second, third
 
         def whole(run):
-            parts = [tile_part(sub, run) for sub in subs]
+            parts = [tile_part(sub_of(j, t, steps), run) for j, t in enumerate(tiles)]
             tops = [p[0]() for p in parts]
             stats = [p[1](top) for p, top in zip(parts, tops)]
             for p, stat in zip(parts, stats):
@@ -195,7 +195,15 @@
         def looped():
             ot[...] = jnp.zeros_like(ot)
             qt[...] = jnp.zeros_like(qt)
-            whole(lambda body, carry: lax.fori_loop(0, steps, body, carry))
+            for j, t in enumerate(tiles):
+                turns = (step_count(t) + 1) // 2
+
+                def run(body, carry, turns=turns):
+                    two = lambda i, c: body(2 * i + 1, body(2 * i, c))
+                    return lax.fori_loop(0, turns, two, carry)
+
+                first, second, third = tile_part(sub_of(j, t, 2 * turns), run)
+                third(second(first()))
 
         lax.switch(
             jnp.minimum(steps - 1, UNROLLED), [unrolled(c + 1) for c in range(UNROLLED)] + [looped]

time: 167 us -> 164 us (0.982)
  waiting for transfers between devices: 82 us -> 71.2 us
  Pallas kernels: 48.7 us -> 55.4 us
    ppermute x4, waiting for transfers between devices: 34.8 us -> 24 us  [shifted(): lax.ppermute(value, 'img', [(s, s + steps) for s in range(leading, last)])]
    pallas_call x1, Pallas kernels: 33.9 us -> 40.6 us  [attend(): pl.pallas_call(attend_kernel, out_shape=(jax.ShapeDtypeStruct((GROUP, 2 *...]
where the time goes in v4:
time: 164 us; the launch traced here: 161 us
  waiting for transfers between devices  71.2 us (43%)
  Pallas kernels  55.4 us (34%)
  starting transfers between devices  27.8 us (17%)
  local copies, waits for them, and re-layouts  3.78 us (2%)
  other arithmetic  2.04 us (1%)
    all_to_all x4, waiting for transfers between devices, exchange(): return lax.all_to_all(x, 'img', 0, 0, axis_index_groups=group_lists())  47.2 us
    pallas_call x1, Pallas kernels, attend(): pl.pallas_call(attend_kernel, out_shape=(jax.ShapeDtypeStruct((GROUP, 2 *...  40.6 us
    ppermute x4, waiting for transfers between devices, shifted(): lax.ppermute(value, 'img', [(s, s + steps) for s in range(leading, last)])  24 us
    all_to_all x4, starting transfers between devices, exchange(): return lax.all_to_all(x, 'img', 0, 0, axis_index_groups=group_lists())  16.1 us
    ppermute x4, starting transfers between devices, shifted(): lax.ppermute(value, 'img', [(s, s + steps) for s in range(leading, last)])  11.7 us
    pallas_call x2, Pallas kernels, unpack(): pl.pallas_call(unpack_kernel, out_shape=(flat, flat), cost_estimate=pl.Co...  5.99 us
    pallas_call x2, Pallas kernels, pack(): pl.pallas_call(kernel, out_shape=jax.ShapeDtypeStruct((GROUP, rows, LANES...  5.68 us
  transfers between devices with their start and end apart: 8, of which 7 were waited for; matrix products, arithmetic and copies ran while one was open for 1% of the time, Pallas kernels for 5%

profile of v4, /device:TPU:38, one launch (start us, length us, event | category | flops | bytes accessed | tf_op | source)
XLA Modules:
  0.0 160.9 jit_solution(5808603015751443136)
XLA Ops:
  0.6 3.5 %pack.2 = bf16[8,1168,128]{2,1,0:T(8,128)(2,1)} custom-call(bf16[384,1024]{1,0:T(8,128)(2,1)} %k_ref.1, bf16[384,1024]{1,0:T(8,128)(2,1)} %v_ref.1, bf16[384,1024]{1,0:T(8,128)(2,1)} %q_ref.1, s32[3,128]{1,0:T(4,128)} %bitcast.7), custom_call_target="tpu_custom_call" | custom-call | bytes 4784128 | tf_op jit(solution)/shard_map/pack/pallas_call | solution.py:274
  4.2 4.5 %all-to-all-start = ((bf16[8,1168,128]{2,1,0:T(8,128)(2,1)}), bf16[8,1168,128]{2,1,0:T(8,128)(2,1)S(1)}, u32[]{:S(2)}, u32[]{:S(2)}) async-start(bf16[8,1168,128]{2,1,0:T(8,128)(2,1)} %pack.2), calls=%async_computation | async-start | bytes 4784128 | tf_op jit(solution)/shard_map/all_to_all | solution.py:321
  8.6 2.2 %pack.3 = bf16[8,384,128]{2,1,0:T(8,128)(2,1)} custom-call(bf16[384,1024]{1,0:T(8,128)(2,1)} %g_ref.1), custom_call_target="tpu_custom_call" | custom-call | bytes 1572864 | tf_op jit(solution)/shard_map/pack/pallas_call | solution.py:274
  10.8 28.2 %all-to-all-done.own_ref = bf16[8,1168,128]{2,1,0:T(8,128)(2,1)S(1)} async-done(((bf16[8,1168,128]{2,1,0:T(8,128)(2,1)}), bf16[8,1168,128]{2,1,0:T(8,128)(2,1)S(1)}, u32[]{:S(2)}, u32[]{:S(2)}) %all-to-all-start) | async-done | bytes 2392096 | tf_op jit(solution)/shard_map/all_to_all | solution.py:321
  39.0 1.0 fusion
  40.6 3.8 %collective-permute-start = (bf16[3,784,128]{2,1,0:T(8,128)(2,1)}, bf16[3,784,128]{2,1,0:T(8,128)(2,1)S(1)}, u32[]{:S(2)}, u32[]{:S(2)}) collective-permute-start(bf16[3,784,128]{2,1,0:T(8,128)(2,1)} %get-tuple-element.28), channel_id=1, source_target_pairs={{0,8},{1,9},{2,10},{3,11},{4,12},{5,13},{6,14},{7,15},{8,16},{9,17... | collective-permute-start | bytes 1806344 | tf_op jit(solution)/shard_map/ppermute | solution.py:40
  44.4 2.0 %collective-permute-start.1 = (bf16[3,784,128]{2,1,0:T(8,128)(2,1)S(1)}, bf16[3,784,128]{2,1,0:T(8,128)(2,1)S(1)}, u32[]{:S(2)}, u32[]{:S(2)}) collective-permute-start(bf16[3,784,128]{2,1,0:T(8,128)(2,1)S(1)} %get-tuple-element.29), channel_id=1, source_target_pairs={{8,0},{9,1},{10,2},{11,3},{12,4},{13,5},{14,6},{15,7},{16,8},{17,9... | collective-permute-start | bytes 1806344 | tf_op jit(solution)/shard_map/ppermute | solution.py:40
  46.5 3.6 %all-to-all-start.1 = ((bf16[8,384,128]{2,1,0:T(8,128)(2,1)}), bf16[8,384,128]{2,1,0:T(8,128)(2,1)S(1)}, u32[]{:S(2)}, u32[]{:S(2)}) async-start(bf16[8,384,128]{2,1,0:T(8,128)(2,1)} %pack.3), calls=%async_computation.1 | async-start | bytes 1572864 | tf_op jit(solution)/shard_map/all_to_all | solution.py:321
  50.8 7.1 %collective-permute-done.left_ref = bf16[3,784,128]{2,1,0:T(8,128)(2,1)S(1)} collective-permute-done((bf16[3,784,128]{2,1,0:T(8,128)(2,1)}, bf16[3,784,128]{2,1,0:T(8,128)(2,1)S(1)}, u32[]{:S(2)}, u32[]{:S(2)}) %collective-permute-start) | collective-permute-done | bytes 602144 | tf_op jit(solution)/shard_map/ppermute | solution.py:40
  57.8 3.3 %collective-permute-done.1.right_ref = bf16[3,784,128]{2,1,0:T(8,128)(2,1)S(1)} collective-permute-done((bf16[3,784,128]{2,1,0:T(8,128)(2,1)S(1)}, bf16[3,784,128]{2,1,0:T(8,128)(2,1)S(1)}, u32[]{:S(2)}, u32[]{:S(2)}) %collective-permute-start.1) | collective-permute-done | bytes 602144 | tf_op jit(solution)/shard_map/ppermute | solution.py:40
  61.2 0.9 convert_reduce_fusion
  63.1 40.6 %attend.1 = (bf16[8,768,128]{2,1,0:T(8,128)(2,1)}, bf16[2,3072,128]{2,1,0:T(8,128)(2,1)}, bf16[2,1152,128]{2,1,0:T(8,128)(2,1)S(1)}, bf16[2,1152,128]{2,1,0:T(8,128)(2,1)S(1)}) custom-call(s32[24]{0:T(128)S(1)} %get-tuple-element.31.lo_ref, s32[24]{0:T(128)S(1)} %get-tuple-element.30.hi_ref, s32[24,128]{1,0:T(8,128)S(1)} %bitcast.6, s32[24,128]{1,0:T(8,128)S(1)} %bitcast.4, ...), custom_call_target="tpu_custom_call" | custom-call | flops 20000000000 | bytes 12000000 | tf_op jit(solution)/shard_map/attend/pallas_call | solution.py:226
  103.7 3.6 %all-to-all-start.2 = ((bf16[8,768,128]{2,1,0:T(8,128)(2,1)}), bf16[8,768,128]{2,1,0:T(8,128)(2,1)S(1)}, u32[]{:S(2)}, u32[]{:S(2)}) async-start(bf16[8,768,128]{2,1,0:T(8,128)(2,1)} %get-tuple-element.16), calls=%async_computation.2 | async-start | bytes 3145728 | tf_op jit(solution)/shard_map/all_to_all | solution.py:321
  107.3 1.9 %collective-permute-start.2 = (bf16[2,1152,128]{2,1,0:T(8,128)(2,1)S(1)}, bf16[2,1152,128]{2,1,0:T(8,128)(2,1)S(1)}, u32[]{:S(2)}, u32[]{:S(2)}) collective-permute-start(bf16[2,1152,128]{2,1,0:T(8,128)(2,1)S(1)} %get-tuple-element.20), channel_id=1, source_target_pairs={{0,8},{1,9},{2,10},{3,11},{4,12},{5,13},{6,14},{7,15},{8,16},{9,17... | collective-permute-start | bytes 1769480 | tf_op jit(solution)/shard_map/ppermute | solution.py:40
  109.2 4.0 %collective-permute-start.3 = (bf16[2,1152,128]{2,1,0:T(8,128)(2,1)S(1)}, bf16[2,1152,128]{2,1,0:T(8,128)(2,1)S(1)}, u32[]{:S(2)}, u32[]{:S(2)}) collective-permute-start(bf16[2,1152,128]{2,1,0:T(8,128)(2,1)S(1)} %get-tuple-element.21), channel_id=1, source_target_pairs={{8,0},{9,1},{10,2},{11,3},{12,4},{13,5},{14,6},{15,7},{16,8},{17,9... | collective-permute-start | bytes 1769480 | tf_op jit(solution)/shard_map/ppermute | solution.py:40
  113.2 11.6 %collective-permute-done.2.prev_ref = bf16[2,1152,128]{2,1,0:T(8,128)(2,1)S(1)} collective-permute-done((bf16[2,1152,128]{2,1,0:T(8,128)(2,1)S(1)}, bf16[2,1152,128]{2,1,0:T(8,128)(2,1)S(1)}, u32[]{:S(2)}, u32[]{:S(2)}) %collective-permute-start.2) | collective-permute-done | bytes 589856 | tf_op jit(solution)/shard_map/ppermute | solution.py:40
  124.8 1.9 %collective-permute-done.3.next_ref = bf16[2,1152,128]{2,1,0:T(8,128)(2,1)S(1)} collective-permute-done((bf16[2,1152,128]{2,1,0:T(8,128)(2,1)S(1)}, bf16[2,1152,128]{2,1,0:T(8,128)(2,1)S(1)}, u32[]{:S(2)}, u32[]{:S(2)}) %collective-permute-start.3) | collective-permute-done | bytes 589856 | tf_op jit(solution)/shard_map/ppermute | solution.py:40
  126.8 0.8 copy-done.4
  127.6 3.2 %total.1 = bf16[8,768,128]{2,1,0:T(8,128)(2,1)} custom-call(bf16[2,3072,128]{2,1,0:T(8,128)(2,1)} %get-tuple-element.19.own_ref, bf16[2,1152,128]{2,1,0:T(8,128)(2,1)} %copy-done.3, bf16[2,1152,128]{2,1,0:T(8,128)(2,1)} %copy-done.4), custom_call_target="tpu_custom_call" | custom-call | bytes 6000000 | tf_op jit(solution)/shard_map/total/pallas_call | solution.py:312
  130.7 4.5 %all-to-all-start.3 = ((bf16[8,768,128]{2,1,0:T(8,128)(2,1)}), bf16[8,768,128]{2,1,0:T(8,128)(2,1)S(1)}, u32[]{:S(2)}, u32[]{:S(2)}) async-start(bf16[8,768,128]{2,1,0:T(8,128)(2,1)} %total.1), calls=%async_computation.3 | async-start | bytes 3145728 | tf_op jit(solution)/shard_map/all_to_all | solution.py:321
  135.2 3.0 %unpack.2 = (bf16[384,1024]{1,0:T(8,128)(2,1)}, bf16[384,1024]{1,0:T(8,128)(2,1)}) custom-call(bf16[8,768,128]{2,1,0:T(8,128)(2,1)} %copy-done), custom_call_target="tpu_custom_call" | custom-call | bytes 3200000 | tf_op jit(solution)/shard_map/unpack/pallas_call | solution.py:291
  138.2 18.6 %all-to-all-done.3.in_ref = bf16[8,768,128]{2,1,0:T(8,128)(2,1)S(1)} async-done(((bf16[8,768,128]{2,1,0:T(8,128)(2,1)}), bf16[8,768,128]{2,1,0:T(8,128)(2,1)S(1)}, u32[]{:S(2)}, u32[]{:S(2)}) %all-to-all-start.3) | async-done | bytes 1572896 | tf_op jit(solution)/shard_map/all_to_all | solution.py:321
  156.8 1.2 copy-done.1
  157.9 3.0 %unpack.3 = (bf16[384,1024]{1,0:T(8,128)(2,1)}, bf16[384,1024]{1,0:T(8,128)(2,1)}) custom-call(bf16[8,768,128]{2,1,0:T(8,128)(2,1)} %copy-done.1), custom_call_target="tpu_custom_call" | custom-call | bytes 3200000 | tf_op jit(solution)/shard_map/unpack/pallas_call | solution.py:291
  (19 shorter events, 2.4 us)
Async XLA Ops:
  4.2 34.8 %all-to-all-start = ((bf16[8,1168,128]{2,1,0:T(8,128)(2,1)}), bf16[8,1168,128]{2,1,0:T(8,128)(2,1)S(1)}, u32[]{:S(2)}, u32[]{:S(2)}) async-start(bf16[8,1168,128]{2,1,0:T(8,128)(2,1)} %pack.2), calls=%async_computation | async-start | bytes 4784128 | tf_op jit(solution)/shard_map/all_to_all | solution.py:321
  39.0 1.6 copy-start.2
  40.6 17.2 %collective-permute-start = (bf16[3,784,128]{2,1,0:T(8,128)(2,1)}, bf16[3,784,128]{2,1,0:T(8,128)(2,1)S(1)}, u32[]{:S(2)}, u32[]{:S(2)}) collective-permute-start(bf16[3,784,128]{2,1,0:T(8,128)(2,1)} %get-tuple-element.28), channel_id=1, source_target_pairs={{0,8},{1,9},{2,10},{3,11},{4,12},{5,13},{6,14},{7,15},{8,16},{9,17... | collective-permute-start | bytes 1806344 | tf_op jit(solution)/shard_map/ppermute | solution.py:40
  44.4 16.7 %collective-permute-start.1 = (bf16[3,784,128]{2,1,0:T(8,128)(2,1)S(1)}, bf16[3,784,128]{2,1,0:T(8,128)(2,1)S(1)}, u32[]{:S(2)}, u32[]{:S(2)}) collective-permute-start(bf16[3,784,128]{2,1,0:T(8,128)(2,1)S(1)} %get-tuple-element.29), channel_id=1, source_target_pairs={{8,0},{9,1},{10,2},{11,3},{12,4},{13,5},{14,6},{15,7},{16,8},{17,9... | collective-permute-start | bytes 1806344 | tf_op jit(solution)/shard_map/ppermute | solution.py:40
  46.5 16.6 %all-to-all-start.1 = ((bf16[8,384,128]{2,1,0:T(8,128)(2,1)}), bf16[8,384,128]{2,1,0:T(8,128)(2,1)S(1)}, u32[]{:S(2)}, u32[]{:S(2)}) async-start(bf16[8,384,128]{2,1,0:T(8,128)(2,1)} %pack.3), calls=%async_computation.1 | async-start | bytes 1572864 | tf_op jit(solution)/shard_map/all_to_all | solution.py:321
  103.7 27.0 %all-to-all-start.2 = ((bf16[8,768,128]{2,1,0:T(8,128)(2,1)}), bf16[8,768,128]{2,1,0:T(8,128)(2,1)S(1)}, u32[]{:S(2)}, u32[]{:S(2)}) async-start(bf16[8,768,128]{2,1,0:T(8,128)(2,1)} %get-tuple-element.16), calls=%async_computation.2 | async-start | bytes 3145728 | tf_op jit(solution)/shard_map/all_to_all | solution.py:321
  107.3 17.5 %collective-permute-start.2 = (bf16[2,1152,128]{2,1,0:T(8,128)(2,1)S(1)}, bf16[2,1152,128]{2,1,0:T(8,128)(2,1)S(1)}, u32[]{:S(2)}, u32[]{:S(2)}) collective-permute-start(bf16[2,1152,128]{2,1,0:T(8,128)(2,1)S(1)} %get-tuple-element.20), channel_id=1, source_target_pairs={{0,8},{1,9},{2,10},{3,11},{4,12},{5,13},{6,14},{7,15},{8,16},{9,17... | collective-permute-start | bytes 1769480 | tf_op jit(solution)/shard_map/ppermute | solution.py:40
  109.2 17.5 %collective-permute-start.3 = (bf16[2,1152,128]{2,1,0:T(8,128)(2,1)S(1)}, bf16[2,1152,128]{2,1,0:T(8,128)(2,1)S(1)}, u32[]{:S(2)}, u32[]{:S(2)}) collective-permute-start(bf16[2,1152,128]{2,1,0:T(8,128)(2,1)S(1)} %get-tuple-element.21), channel_id=1, source_target_pairs={{8,0},{9,1},{10,2},{11,3},{12,4},{13,5},{14,6},{15,7},{16,8},{17,9... | collective-permute-start | bytes 1769480 | tf_op jit(solution)/shard_map/ppermute | solution.py:40
  124.8 1.9 %copy-start.3 = (bf16[2,1152,128]{2,1,0:T(8,128)(2,1)}, bf16[2,1152,128]{2,1,0:T(8,128)(2,1)S(1)}, u32[]{:S(2)}) copy-start(bf16[2,1152,128]{2,1,0:T(8,128)(2,1)S(1)} %collective-permute-done.2.prev_ref) | copy-start | bytes 1769476
  126.8 0.8 copy-start.4
  130.7 4.5 %copy-start = (bf16[8,768,128]{2,1,0:T(8,128)(2,1)}, bf16[8,768,128]{2,1,0:T(8,128)(2,1)S(1)}, u32[]{:S(2)}) copy-start(bf16[8,768,128]{2,1,0:T(8,128)(2,1)S(1)} %all-to-all-done.2.in_ref) | copy-start | bytes 4718596
  130.7 26.1 %all-to-all-start.3 = ((bf16[8,768,128]{2,1,0:T(8,128)(2,1)}), bf16[8,768,128]{2,1,0:T(8,128)(2,1)S(1)}, u32[]{:S(2)}, u32[]{:S(2)}) async-start(bf16[8,768,128]{2,1,0:T(8,128)(2,1)} %total.1), calls=%async_computation.3 | async-start | bytes 3145728 | tf_op jit(solution)/shard_map/all_to_all | solution.py:321
  156.8 1.2 copy-start.1

commit v5 on v4

--- a/solution.py
+++ b/solution.py
@@ -196,13 +196,13 @@
             ot[...] = jnp.zeros_like(ot)
             qt[...] = jnp.zeros_like(qt)
             for j, t in enumerate(tiles):
-                turns = (step_count(t) + 1) // 2
+                turns = (step_count(t) + 2) // 3
 
                 def run(body, carry, turns=turns):
-                    two = lambda i, c: body(2 * i + 1, body(2 * i, c))
-                    return lax.fori_loop(0, turns, two, carry)
-
-                first, second, third = tile_part(sub_of(j, t, 2 * turns), run)
+                    three = lambda i, c: body(3 * i + 2, body(3 * i + 1, body(3 * i, c)))
+                    return lax.fori_loop(0, turns, three, carry)
+
+                first, second, third = tile_part(sub_of(j, t, 3 * turns), run)
                 third(second(first()))
 
         lax.switch(

time: 164 us -> 166 us (1.012); the launches traced: 161 us -> 165 us
  starting transfers between devices: 27.8 us -> 39.5 us
  Pallas kernels: 55.4 us -> 46 us
  waiting for transfers between devices: 71.2 us -> 72.9 us
    ppermute x4, starting transfers between devices: 11.7 us -> 23.4 us  [shifted(): lax.ppermute(value, 'img', [(s, s + steps) for s in range(leading, last)])]
    pallas_call x1, Pallas kernels: 40.6 us -> 31.1 us  [attend(): pl.pallas_call(attend_kernel, out_shape=(jax.ShapeDtypeStruct((GROUP, 2 *...]
    ppermute x4, waiting for transfers between devices: 24 us -> 25.7 us  [shifted(): lax.ppermute(value, 'img', [(s, s + steps) for s in range(leading, last)])]
where the time goes in v5:
time: 166 us; the launch traced here: 165 us
  waiting for transfers between devices  72.9 us (44%)
  Pallas kernels  46 us (28%)
  starting transfers between devices  39.5 us (24%)
  local copies, waits for them, and re-layouts  3.78 us (2%)
  other arithmetic  2.04 us (1%)
    all_to_all x4, waiting for transfers between devices, exchange(): return lax.all_to_all(x, 'img', 0, 0, axis_index_groups=group_lists())  47.2 us
    pallas_call x1, Pallas kernels, attend(): pl.pallas_call(attend_kernel, out_shape=(jax.ShapeDtypeStruct((GROUP, 2 *...  31.1 us
    ppermute x4, waiting for transfers between devices, shifted(): lax.ppermute(value, 'img', [(s, s + steps) for s in range(leading, last)])  25.7 us
    ppermute x4, starting transfers between devices, shifted(): lax.ppermute(value, 'img', [(s, s + steps) for s in range(leading, last)])  23.4 us
    all_to_all x4, starting transfers between devices, exchange(): return lax.all_to_all(x, 'img', 0, 0, axis_index_groups=group_lists())  16.1 us
    pallas_call x2, Pallas kernels, unpack(): pl.pallas_call(unpack_kernel, out_shape=(flat, flat), cost_estimate=pl.Co...  5.99 us
    pallas_call x2, Pallas kernels, pack(): pl.pallas_call(kernel, out_shape=jax.ShapeDtypeStruct((GROUP, rows, LANES...  5.68 us
  transfers between devices with their start and end apart: 8, of which 7 were waited for; matrix products, arithmetic and copies ran while one was open for 1% of the time, Pallas kernels for 5%

profile of v5, /device:TPU:38, one launch (start us, length us, event | category | flops | bytes accessed | tf_op | source)
XLA Modules:
  0.0 164.9 jit_solution(3520012066272801050)
XLA Ops:
  0.6 3.5 %pack.2 = bf16[8,1168,128]{2,1,0:T(8,128)(2,1)} custom-call(bf16[384,1024]{1,0:T(8,128)(2,1)} %k_ref.1, bf16[384,1024]{1,0:T(8,128)(2,1)} %v_ref.1, bf16[384,1024]{1,0:T(8,128)(2,1)} %q_ref.1, s32[3,128]{1,0:T(4,128)} %bitcast.7), custom_call_target="tpu_custom_call" | custom-call | bytes 4784128 | tf_op jit(solution)/shard_map/pack/pallas_call | solution.py:274
  4.2 4.5 %all-to-all-start = ((bf16[8,1168,128]{2,1,0:T(8,128)(2,1)}), bf16[8,1168,128]{2,1,0:T(8,128)(2,1)S(1)}, u32[]{:S(2)}, u32[]{:S(2)}) async-start(bf16[8,1168,128]{2,1,0:T(8,128)(2,1)} %pack.2), calls=%async_computation | async-start | bytes 4784128 | tf_op jit(solution)/shard_map/all_to_all | solution.py:321
  8.6 2.2 %pack.3 = bf16[8,384,128]{2,1,0:T(8,128)(2,1)} custom-call(bf16[384,1024]{1,0:T(8,128)(2,1)} %g_ref.1), custom_call_target="tpu_custom_call" | custom-call | bytes 1572864 | tf_op jit(solution)/shard_map/pack/pallas_call | solution.py:274
  10.8 28.2 %all-to-all-done.own_ref = bf16[8,1168,128]{2,1,0:T(8,128)(2,1)S(1)} async-done(((bf16[8,1168,128]{2,1,0:T(8,128)(2,1)}), bf16[8,1168,128]{2,1,0:T(8,128)(2,1)S(1)}, u32[]{:S(2)}, u32[]{:S(2)}) %all-to-all-start) | async-done | bytes 2392096 | tf_op jit(solution)/shard_map/all_to_all | solution.py:321
  39.0 1.0 fusion
  40.6 3.8 %collective-permute-start = (bf16[3,784,128]{2,1,0:T(8,128)(2,1)}, bf16[3,784,128]{2,1,0:T(8,128)(2,1)S(1)}, u32[]{:S(2)}, u32[]{:S(2)}) collective-permute-start(bf16[3,784,128]{2,1,0:T(8,128)(2,1)} %get-tuple-element.28), channel_id=1, source_target_pairs={{0,8},{1,9},{2,10},{3,11},{4,12},{5,13},{6,14},{7,15},{8,16},{9,17... | collective-permute-start | bytes 1806344 | tf_op jit(solution)/shard_map/ppermute | solution.py:40
  44.4 2.0 %collective-permute-start.1 = (bf16[3,784,128]{2,1,0:T(8,128)(2,1)S(1)}, bf16[3,784,128]{2,1,0:T(8,128)(2,1)S(1)}, u32[]{:S(2)}, u32[]{:S(2)}) collective-permute-start(bf16[3,784,128]{2,1,0:T(8,128)(2,1)S(1)} %get-tuple-element.29), channel_id=1, source_target_pairs={{8,0},{9,1},{10,2},{11,3},{12,4},{13,5},{14,6},{15,7},{16,8},{17,9... | collective-permute-start | bytes 1806344 | tf_op jit(solution)/shard_map/ppermute | solution.py:40
  46.5 3.6 %all-to-all-start.1 = ((bf16[8,384,128]{2,1,0:T(8,128)(2,1)}), bf16[8,384,128]{2,1,0:T(8,128)(2,1)S(1)}, u32[]{:S(2)}, u32[]{:S(2)}) async-start(bf16[8,384,128]{2,1,0:T(8,128)(2,1)} %pack.3), calls=%async_computation.1 | async-start | bytes 1572864 | tf_op jit(solution)/shard_map/all_to_all | solution.py:321
  50.8 7.1 %collective-permute-done.left_ref = bf16[3,784,128]{2,1,0:T(8,128)(2,1)S(1)} collective-permute-done((bf16[3,784,128]{2,1,0:T(8,128)(2,1)}, bf16[3,784,128]{2,1,0:T(8,128)(2,1)S(1)}, u32[]{:S(2)}, u32[]{:S(2)}) %collective-permute-start) | collective-permute-done | bytes 602144 | tf_op jit(solution)/shard_map/ppermute | solution.py:40
  57.8 3.3 %collective-permute-done.1.right_ref = bf16[3,784,128]{2,1,0:T(8,128)(2,1)S(1)} collective-permute-done((bf16[3,784,128]{2,1,0:T(8,128)(2,1)S(1)}, bf16[3,784,128]{2,1,0:T(8,128)(2,1)S(1)}, u32[]{:S(2)}, u32[]{:S(2)}) %collective-permute-start.1) | collective-permute-done | bytes 602144 | tf_op jit(solution)/shard_map/ppermute | solution.py:40
  61.2 0.9 convert_reduce_fusion
  63.1 31.1 %attend.1 = (bf16[8,768,128]{2,1,0:T(8,128)(2,1)}, bf16[2,3072,128]{2,1,0:T(8,128)(2,1)}, bf16[2,1152,128]{2,1,0:T(8,128)(2,1)S(1)}, bf16[2,1152,128]{2,1,0:T(8,128)(2,1)S(1)}) custom-call(s32[24]{0:T(128)S(1)} %get-tuple-element.31.lo_ref, s32[24]{0:T(128)S(1)} %get-tuple-element.30.hi_ref, s32[24,128]{1,0:T(8,128)S(1)} %bitcast.6, s32[24,128]{1,0:T(8,128)S(1)} %bitcast.4, ...), custom_call_target="tpu_custom_call" | custom-call | flops 20000000000 | bytes 12000000 | tf_op jit(solution)/shard_map/attend/pallas_call | solution.py:226
  94.2 3.6 %all-to-all-start.2 = ((bf16[8,768,128]{2,1,0:T(8,128)(2,1)}), bf16[8,768,128]{2,1,0:T(8,128)(2,1)S(1)}, u32[]{:S(2)}, u32[]{:S(2)}) async-start(bf16[8,768,128]{2,1,0:T(8,128)(2,1)} %get-tuple-element.16), calls=%async_computation.2 | async-start | bytes 3145728 | tf_op jit(solution)/shard_map/all_to_all | solution.py:321
  97.8 15.6 %collective-permute-start.2 = (bf16[2,1152,128]{2,1,0:T(8,128)(2,1)S(1)}, bf16[2,1152,128]{2,1,0:T(8,128)(2,1)S(1)}, u32[]{:S(2)}, u32[]{:S(2)}) collective-permute-start(bf16[2,1152,128]{2,1,0:T(8,128)(2,1)S(1)} %get-tuple-element.20), channel_id=1, source_target_pairs={{0,8},{1,9},{2,10},{3,11},{4,12},{5,13},{6,14},{7,15},{8,16},{9,17... | collective-permute-start | bytes 1769480 | tf_op jit(solution)/shard_map/ppermute | solution.py:40
  113.5 1.9 %collective-permute-start.3 = (bf16[2,1152,128]{2,1,0:T(8,128)(2,1)S(1)}, bf16[2,1152,128]{2,1,0:T(8,128)(2,1)S(1)}, u32[]{:S(2)}, u32[]{:S(2)}) collective-permute-start(bf16[2,1152,128]{2,1,0:T(8,128)(2,1)S(1)} %get-tuple-element.21), channel_id=1, source_target_pairs={{8,0},{9,1},{10,2},{11,3},{12,4},{13,5},{14,6},{15,7},{16,8},{17,9... | collective-permute-start | bytes 1769480 | tf_op jit(solution)/shard_map/ppermute | solution.py:40
  115.4 11.2 %collective-permute-done.2.prev_ref = bf16[2,1152,128]{2,1,0:T(8,128)(2,1)S(1)} collective-permute-done((bf16[2,1152,128]{2,1,0:T(8,128)(2,1)S(1)}, bf16[2,1152,128]{2,1,0:T(8,128)(2,1)S(1)}, u32[]{:S(2)}, u32[]{:S(2)}) %collective-permute-start.2) | collective-permute-done | bytes 589856 | tf_op jit(solution)/shard_map/ppermute | solution.py:40
  126.6 4.1 %collective-permute-done.3.next_ref = bf16[2,1152,128]{2,1,0:T(8,128)(2,1)S(1)} collective-permute-done((bf16[2,1152,128]{2,1,0:T(8,128)(2,1)S(1)}, bf16[2,1152,128]{2,1,0:T(8,128)(2,1)S(1)}, u32[]{:S(2)}, u32[]{:S(2)}) %collective-permute-start.3) | collective-permute-done | bytes 589856 | tf_op jit(solution)/shard_map/ppermute | solution.py:40
  130.7 0.8 copy-done.4
  131.5 3.2 %total.1 = bf16[8,768,128]{2,1,0:T(8,128)(2,1)} custom-call(bf16[2,3072,128]{2,1,0:T(8,128)(2,1)} %get-tuple-element.19.own_ref, bf16[2,1152,128]{2,1,0:T(8,128)(2,1)} %copy-done.3, bf16[2,1152,128]{2,1,0:T(8,128)(2,1)} %copy-done.4), custom_call_target="tpu_custom_call" | custom-call | bytes 6000000 | tf_op jit(solution)/shard_map/total/pallas_call | solution.py:312
  134.7 4.5 %all-to-all-start.3 = ((bf16[8,768,128]{2,1,0:T(8,128)(2,1)}), bf16[8,768,128]{2,1,0:T(8,128)(2,1)S(1)}, u32[]{:S(2)}, u32[]{:S(2)}) async-start(bf16[8,768,128]{2,1,0:T(8,128)(2,1)} %total.1), calls=%async_computation.3 | async-start | bytes 3145728 | tf_op jit(solution)/shard_map/all_to_all | solution.py:321
  139.1 3.0 %unpack.2 = (bf16[384,1024]{1,0:T(8,128)(2,1)}, bf16[384,1024]{1,0:T(8,128)(2,1)}) custom-call(bf16[8,768,128]{2,1,0:T(8,128)(2,1)} %copy-done), custom_call_target="tpu_custom_call" | custom-call | bytes 3200000 | tf_op jit(solution)/shard_map/unpack/pallas_call | solution.py:291
  142.1 18.6 %all-to-all-done.3.in_ref = bf16[8,768,128]{2,1,0:T(8,128)(2,1)S(1)} async-done(((bf16[8,768,128]{2,1,0:T(8,128)(2,1)}), bf16[8,768,128]{2,1,0:T(8,128)(2,1)S(1)}, u32[]{:S(2)}, u32[]{:S(2)}) %all-to-all-start.3) | async-done | bytes 1572896 | tf_op jit(solution)/shard_map/all_to_all | solution.py:321
  160.7 1.2 copy-done.1
  161.9 3.0 %unpack.3 = (bf16[384,1024]{1,0:T(8,128)(2,1)}, bf16[384,1024]{1,0:T(8,128)(2,1)}) custom-call(bf16[8,768,128]{2,1,0:T(8,128)(2,1)} %copy-done.1), custom_call_target="tpu_custom_call" | custom-call | bytes 3200000 | tf_op jit(solution)/shard_map/unpack/pallas_call | solution.py:291
  (19 shorter events, 2.4 us)
Async XLA Ops:
  4.2 34.8 %all-to-all-start = ((bf16[8,1168,128]{2,1,0:T(8,128)(2,1)}), bf16[8,1168,128]{2,1,0:T(8,128)(2,1)S(1)}, u32[]{:S(2)}, u32[]{:S(2)}) async-start(bf16[8,1168,128]{2,1,0:T(8,128)(2,1)} %pack.2), calls=%async_computation | async-start | bytes 4784128 | tf_op jit(solution)/shard_map/all_to_all | solution.py:321
  39.0 1.6 copy-start.2
  40.6 17.2 %collective-permute-start = (bf16[3,784,128]{2,1,0:T(8,128)(2,1)}, bf16[3,784,128]{2,1,0:T(8,128)(2,1)S(1)}, u32[]{:S(2)}, u32[]{:S(2)}) collective-permute-start(bf16[3,784,128]{2,1,0:T(8,128)(2,1)} %get-tuple-element.28), channel_id=1, source_target_pairs={{0,8},{1,9},{2,10},{3,11},{4,12},{5,13},{6,14},{7,15},{8,16},{9,17... | collective-permute-start | bytes 1806344 | tf_op jit(solution)/shard_map/ppermute | solution.py:40
  44.4 16.7 %collective-permute-start.1 = (bf16[3,784,128]{2,1,0:T(8,128)(2,1)S(1)}, bf16[3,784,128]{2,1,0:T(8,128)(2,1)S(1)}, u32[]{:S(2)}, u32[]{:S(2)}) collective-permute-start(bf16[3,784,128]{2,1,0:T(8,128)(2,1)S(1)} %get-tuple-element.29), channel_id=1, source_target_pairs={{8,0},{9,1},{10,2},{11,3},{12,4},{13,5},{14,6},{15,7},{16,8},{17,9... | collective-permute-start | bytes 1806344 | tf_op jit(solution)/shard_map/ppermute | solution.py:40
  46.5 16.6 %all-to-all-start.1 = ((bf16[8,384,128]{2,1,0:T(8,128)(2,1)}), bf16[8,384,128]{2,1,0:T(8,128)(2,1)S(1)}, u32[]{:S(2)}, u32[]{:S(2)}) async-start(bf16[8,384,128]{2,1,0:T(8,128)(2,1)} %pack.3), calls=%async_computation.1 | async-start | bytes 1572864 | tf_op jit(solution)/shard_map/all_to_all | solution.py:321
  94.2 40.4 %all-to-all-start.2 = ((bf16[8,768,128]{2,1,0:T(8,128)(2,1)}), bf16[8,768,128]{2,1,0:T(8,128)(2,1)S(1)}, u32[]{:S(2)}, u32[]{:S(2)}) async-start(bf16[8,768,128]{2,1,0:T(8,128)(2,1)} %get-tuple-element.16), calls=%async_computation.2 | async-start | bytes 3145728 | tf_op jit(solution)/shard_map/all_to_all | solution.py:321
  97.8 28.7 %collective-permute-start.2 = (bf16[2,1152,128]{2,1,0:T(8,128)(2,1)S(1)}, bf16[2,1152,128]{2,1,0:T(8,128)(2,1)S(1)}, u32[]{:S(2)}, u32[]{:S(2)}) collective-permute-start(bf16[2,1152,128]{2,1,0:T(8,128)(2,1)S(1)} %get-tuple-element.20), channel_id=1, source_target_pairs={{0,8},{1,9},{2,10},{3,11},{4,12},{5,13},{6,14},{7,15},{8,16},{9,17... | collective-permute-start | bytes 1769480 | tf_op jit(solution)/shard_map/ppermute | solution.py:40
  113.5 17.2 %collective-permute-start.3 = (bf16[2,1152,128]{2,1,0:T(8,128)(2,1)S(1)}, bf16[2,1152,128]{2,1,0:T(8,128)(2,1)S(1)}, u32[]{:S(2)}, u32[]{:S(2)}) collective-permute-start(bf16[2,1152,128]{2,1,0:T(8,128)(2,1)S(1)} %get-tuple-element.21), channel_id=1, source_target_pairs={{8,0},{9,1},{10,2},{11,3},{12,4},{13,5},{14,6},{15,7},{16,8},{17,9... | collective-permute-start | bytes 1769480 | tf_op jit(solution)/shard_map/ppermute | solution.py:40
  126.6 4.1 %copy-start.3 = (bf16[2,1152,128]{2,1,0:T(8,128)(2,1)}, bf16[2,1152,128]{2,1,0:T(8,128)(2,1)S(1)}, u32[]{:S(2)}) copy-start(bf16[2,1152,128]{2,1,0:T(8,128)(2,1)S(1)} %collective-permute-done.2.prev_ref) | copy-start | bytes 1769476
  130.7 0.8 copy-start.4
  134.6 4.5 %copy-start = (bf16[8,768,128]{2,1,0:T(8,128)(2,1)}, bf16[8,768,128]{2,1,0:T(8,128)(2,1)S(1)}, u32[]{:S(2)}) copy-start(bf16[8,768,128]{2,1,0:T(8,128)(2,1)S(1)} %all-to-all-done.2.in_ref) | copy-start | bytes 4718596
  134.7 26.1 %all-to-all-start.3 = ((bf16[8,768,128]{2,1,0:T(8,128)(2,1)}), bf16[8,768,128]{2,1,0:T(8,128)(2,1)S(1)}, u32[]{:S(2)}, u32[]{:S(2)}) async-start(bf16[8,768,128]{2,1,0:T(8,128)(2,1)} %total.1), calls=%async_computation.3 | async-start | bytes 3145728 | tf_op jit(solution)/shard_map/all_to_all | solution.py:321
  160.7 1.2 copy-start.1
